TPU v7x, 256 devices: a whole 4x4x8 slice. The times are simulated.
256 devices in a mesh: group: 8 (over z), blk: 32 (over x, y, core).
Axes of the slice: x: 4, y: 4, z: 8, core: 2. Of those that a mesh axis runs over, the one named last changes fastest.
Arguments:
- image_a: float32 [3, 2048, 8192], P(None, 'group', 'blk'), may hold values from -6 to 6
- image_b: float32 [3, 2048, 8192], P(None, 'group', 'blk'), may hold values from -6 to 6
- initial: float32 [3, 2048, 8192], P(None, 'group', 'blk'), may hold values from -6 to 6
- coverage: int32 [8, 32], P('group', 'blk'), may hold values 0 or 1
- seam_label: int32 [8, 32], P('group', 'blk'), may hold values from 0 to 1
Outputs:
- blended: float32 [3, 2048, 8192], P(None, 'group', 'blk')
All inputs are finite; a program needn't handle non-finite values. No bound on the sum of `coverage` on one device may be relied on, other than what follows from the above.
Results may differ from a plain program's by a relative error of at most 0.00003.
Values sent between devices are 32-bit elements; how exact they have to be, the bound alone decides.
A program may use at most 128 MiB of HBM per device.

v0:
```python
import jax
import jax.numpy as jnp
from jax import lax
from jax.sharding import PartitionSpec as P

BS = 256
LEVELS = 4
NU = 2
COARSE = 4


RELAX = 0.8


def padded_2(x, sides, width):
    edges = {}
    for axis, dim in sides:
        size, length = (lax.axis_size(axis), x.shape[dim])
        up = [(i, (i + 1) % size) for i in range(size - 1)]
        last = lax.slice_in_dim(x, length - width, length, axis=dim)
        leading = lax.slice_in_dim(x, 0, width, axis=dim)
        edges[dim] = (
            lax.ppermute(last, axis, up),
            lax.ppermute(leading, axis, [(b, a) for a, b in up]),
        )
    done = []
    for _, dim in sides:
        low, high = edges[dim]
        around = [(width, width) if d in done else (0, 0) for d in range(x.ndim)]
        x = jnp.concatenate([jnp.pad(low, around), x, jnp.pad(high, around)], axis=dim)
        done.append(dim)
    return x


def padded_3(cells, sides, width):
    for axis, dim in sides:
        count = lax.axis_size(axis)
        ends = count - 1
        head = lax.slice_in_dim(cells, 0, width, axis=dim)
        tail = lax.slice_in_dim(cells, cells.shape[dim] - width, cells.shape[dim], axis=dim)
        cells = jnp.concatenate(
            [
                lax.ppermute(tail, axis, [(i, (i + 1) % count) for i in range(ends)]),
                cells,
                lax.ppermute(head, axis, [((i + 1) % count, i) for i in range(ends)]),
            ],
            axis=dim,
        )
    return cells


def beside_sum(padded):
    return padded[:, :-2, 1:-1] + padded[:, 2:, 1:-1] + padded[:, 1:-1, :-2] + padded[:, 1:-1, 2:]


def local_rim(field):
    return padded_2(field, (("group", 1), ("blk", 2)), 1)


def cell_map(table, span):
    return jnp.repeat(jnp.repeat(table, span, 0), span, 1)


def crop(field, margin):
    return field[:, margin:-margin, margin:-margin]


def smooth(approx, source, active, depth_index, sweeps):
    factor = 0.25**depth_index
    start = 0
    approx = RELAX * active * source / (4.0 * factor)
    start = 1
    for sweep in range(start, sweeps):
        approx = approx + RELAX * active * (
            source - factor * (4.0 * approx - beside_sum(local_rim(approx)))
        ) / (4.0 * factor)
    return approx


def shrink(field):
    chans, rows, cols = field.shape
    return field.reshape(chans, rows // 2, 2, cols // 2, 2).mean(axis=(2, 4))


def expand(field):
    return jnp.repeat(jnp.repeat(field, 2, 1), 2, 2)


def wide_sweep(approx_wide, source_wide, active_wide, factor):
    margin = (source_wide.shape[1] - approx_wide.shape[1]) // 2 + 1
    inner = crop(approx_wide, 1)
    source_in = crop(source_wide, margin)
    active_in = crop(active_wide, margin)
    return inner + RELAX * active_in * (
        source_in - factor * (4.0 * inner - beside_sum(approx_wide))
    ) / (4.0 * factor)


def deep_cycle(source, active, depth_index, coarser):
    factor = 0.25**depth_index
    chans = source.shape[0]
    if depth_index == LEVELS - 1:
        return smooth(None, source, active, depth_index, COARSE)
    joined = jnp.concatenate([source, active], 0)
    joined_wide = padded_3(joined, (("group", 1), ("blk", 2)), NU)
    source_wide = joined_wide[0:chans]
    active_wide = joined_wide[chans : chans + 1]
    approx_wide = RELAX * active_wide * source_wide / (4.0 * factor)
    approx_wide = wide_sweep(approx_wide, source_wide, active_wide, factor)
    leftover = active * (source - factor * (4.0 * crop(approx_wide, 1) - beside_sum(approx_wide)))
    approx = crop(approx_wide, 1)
    coarse_fix = coarser(shrink(leftover), depth_index + 1)
    approx = approx + active * expand(coarse_fix)
    approx_wide = padded_3(approx, (("group", 1), ("blk", 2)), NU)
    for sweep in range(NU):
        approx_wide = wide_sweep(approx_wide, source_wide, active_wide, factor)
    return approx_wide


def shards(image_a, image_b, initial, coverage, seam_label):
    stacked = jnp.concatenate([image_a, image_b, initial], 0)
    padded = padded_2(stacked, (("group", 1), ("blk", 2)), 1)
    laplace = 4.0 * stacked - beside_sum(padded)
    chans = image_a.shape[0]
    laplace_a = laplace[0:chans]
    laplace_b = laplace[chans : 2 * chans]
    laplace_x = laplace[2 * chans : 3 * chans]
    labels = cell_map(seam_label, BS)[None]
    guide = jnp.where(labels == 1, laplace_b, laplace_a)

    def active_at(depth_index):
        return cell_map(coverage, BS >> depth_index).astype(jnp.float32)[None]

    def local_cycle(source, active, depth_index):
        return deep_cycle(source, active, depth_index, coarser_local)

    def coarser_local(next_source, next_depth):
        return local_cycle(next_source, active_at(next_depth), next_depth)

    active_top = active_at(0)
    source = active_top * (guide - laplace_x)
    return initial + local_cycle(source, active_top, 0)


def solution(mesh):
    placed = (
        P(None, "group", "blk"),
        P(None, "group", "blk"),
        P(None, "group", "blk"),
        P("group", "blk"),
        P("group", "blk"),
    )
    return jax.shard_map(
        shards, mesh=mesh, in_specs=placed, out_specs=P(None, "group", "blk"), check_vma=False
    )
```

profile of v0, /device:TPU:70, one launch (start us, length us, event | category | flops | bytes accessed | tf_op | source)
XLA Modules:
  0.0 366.3 jit_solution(14289786886239237261)
XLA Ops:
  8.9 3.8 %collective-permute-start = (f32[9,1,256]{2,1,0:T(1,128)S(1)}, f32[9,1,256]{2,1,0:T(1,128)S(1)}, u32[]{:S(2)}, u32[]{:S(2)}) collective-permute-start(f32[9,1,256]{2,1,0:T(1,128)S(1)} %copy.30), channel_id=1, source_target_pairs={{0,32},{32,64},{64,96},{96,128},{128,160},{160,192},{192,224},{1,3... | collective-permute-start | bytes 27656 | tf_op jit(solution)/shard_map/ppermute | solution.py:23
  18.3 5.8 %collective-permute-start.3 = (f32[9,256,1]{1,2,0:T(1,128)S(1)}, f32[9,256,1]{1,2,0:T(1,128)S(1)}, u32[]{:S(2)}, u32[]{:S(2)}) collective-permute-start(f32[9,256,1]{1,2,0:T(1,128)S(1)} %get-tuple-element.6), channel_id=1, source_target_pairs={{1,0},{2,1},{3,2},{4,3},{5,4},{6,5},{7,6},{8,7},{9,8},{10,9},{11,1... | collective-permute-start | bytes 27656 | tf_op jit(solution)/shard_map/ppermute | solution.py:24
  28.3 7.1 %fusion.2 = f32[9,256,256]{1,2,0:T(8,128)S(1)} fusion(f32[9,256,1]{1,2,0:T(1,128)S(1)} %collective-permute-done.3, f32[9,1,256]{1,2,0:T(8,128)} %copy.33, f32[9,1,256]{1,2,0:T(8,128)} %copy.31, f32[3,256,256]{1,2,0:T(8,128)S(1)} %copy.42, f32[3,256,256]{1,2,0:T(8,128)} %copy.28, f32[3,256,256]{1,2,0:T(8,128)} %copy.27, f32[9,256,1]{1,2,0:T(1,128)S(1)} %collective-permute-done.2), kind=kLoop, calls=%fused_computation.3 | loop fusion | flops 17104896 | bytes 4755456 | tf_op jit(solution)/shard_map/sub | solution.py:123
  35.7 4.9 %collective-permute-start.4 = (f32[4,2,256]{1,2,0:T(8,128)S(1)}, f32[4,2,256]{1,2,0:T(8,128)S(1)}, u32[]{:S(2)}, u32[]{:S(2)}) collective-permute-start(f32[4,2,256]{1,2,0:T(8,128)S(1)} %get-tuple-element.15), channel_id=1, source_target_pairs={{0,32},{32,64},{64,96},{96,128},{128,160},{160,192},{192,224},{1,3... | collective-permute-start | bytes 24584 | tf_op jit(solution)/shard_map/ppermute | solution.py:43
  42.7 7.2 %collective-permute-done.4 = f32[4,2,256]{1,2,0:T(8,128)S(1)} collective-permute-done((f32[4,2,256]{1,2,0:T(8,128)S(1)}, f32[4,2,256]{1,2,0:T(8,128)S(1)}, u32[]{:S(2)}, u32[]{:S(2)}) %collective-permute-start.4) | collective-permute-done | bytes 8224 | tf_op jit(solution)/shard_map/ppermute | solution.py:43
  49.9 5.6 %collective-permute-done.5 = f32[4,2,256]{1,2,0:T(8,128)S(1)} collective-permute-done((f32[4,2,256]{1,2,0:T(8,128)S(1)}, f32[4,2,256]{1,2,0:T(8,128)S(1)}, u32[]{:S(2)}, u32[]{:S(2)}) %collective-permute-start.5) | collective-permute-done | bytes 8224 | tf_op jit(solution)/shard_map/ppermute | solution.py:45
  57.5 5.8 %collective-permute-start.7 = (f32[4,260,2]{1,2,0:T(2,128)S(1)}, f32[4,260,2]{1,2,0:T(2,128)S(1)}, u32[]{:S(2)}, u32[]{:S(2)}) collective-permute-start(f32[4,260,2]{1,2,0:T(2,128)S(1)} %get-tuple-element.10), channel_id=1, source_target_pairs={{1,0},{2,1},{3,2},{4,3},{5,4},{6,5},{7,6},{8,7},{9,8},{10,9},{11,1... | collective-permute-start | bytes 24968 | tf_op jit(solution)/shard_map/ppermute | solution.py:45
  71.0 2.3 copy.36
  73.3 52.4 %reshape.45 = f32[3,128,2,128,2]{4,3,2,1,0:T(8,128)} reshape(f32[3,256,256]{2,1,0:T(8,128)} %copy.36) | data formatting | bytes 1572864 | tf_op jit(solution)/shard_map/reshape | solution.py:82
  125.7 19.3 %reduce_sum.27 = f32[3,128,128]{2,1,0:T(8,128)S(1)} reduce(f32[3,128,2,128,2]{4,3,2,1,0:T(8,128)} %reshape.45, f32[]{:T(128)} %constant.21.clone.1), dimensions={2,4}, to_apply=%region_0.1 | reduce | flops 147456 | bytes 983044 | tf_op jit(solution)/shard_map/reduce_sum | solution.py:82
  145.0 4.9 %collective-permute-start.8 = (f32[4,2,128]{2,1,0:T(2,128)S(1)}, f32[4,2,128]{2,1,0:T(2,128)S(1)}, u32[]{:S(2)}, u32[]{:S(2)}) collective-permute-start(f32[4,2,128]{2,1,0:T(2,128)S(1)} %get-tuple-element.23), channel_id=1, source_target_pairs={{0,32},{32,64},{64,96},{96,128},{128,160},{160,192},{192,224},{1,3... | collective-permute-start | bytes 12296 | tf_op jit(solution)/shard_map/ppermute | solution.py:43
  151.8 3.5 collective-permute-done.9
  157.5 5.9 %collective-permute-start.11 = (f32[4,132,2]{2,1,0:T(8,128)S(1)}, f32[4,132,2]{2,1,0:T(8,128)S(1)}, u32[]{:S(2)}, u32[]{:S(2)}) collective-permute-start(f32[4,132,2]{2,1,0:T(8,128)S(1)} %get-tuple-element.18), channel_id=1, source_target_pairs={{1,0},{2,1},{3,2},{4,3},{5,4},{6,5},{7,6},{8,7},{9,8},{10,9},{11,1... | collective-permute-start | bytes 12680 | tf_op jit(solution)/shard_map/ppermute | solution.py:45
  170.1 14.7 %reshape.46 = f32[3,64,2,64,2]{4,3,2,1,0:T(8,128)} reshape(f32[3,128,128]{2,1,0:T(8,128)} %fusion.52) | data formatting | bytes 393216 | tf_op jit(solution)/shard_map/reshape | solution.py:82
  184.9 6.3 %reduce_sum.28 = f32[3,64,64]{2,1,0:T(8,128)S(1)} reduce(f32[3,64,2,64,2]{4,3,2,1,0:T(8,128)} %reshape.46, f32[]{:T(128)} %constant.21.clone.1), dimensions={2,4}, to_apply=%region_1.2 | reduce | flops 36864 | bytes 245764 | tf_op jit(solution)/shard_map/reduce_sum | solution.py:82
  191.2 3.1 collective-permute-start.12
  194.4 2.7 collective-permute-start.13
  197.1 2.7 collective-permute-done.13
  202.6 5.8 %collective-permute-start.15 = (f32[4,68,2]{2,1,0:T(8,128)}, f32[4,68,2]{2,1,0:T(8,128)}, u32[]{:S(2)}, u32[]{:S(2)}) collective-permute-start(f32[4,68,2]{2,1,0:T(8,128)} %get-tuple-element.26), channel_id=1, source_target_pairs={{1,0},{2,1},{3,2},{4,3},{5,4},{6,5},{7,6},{8,7},{9,8},{10,9},{11,1... | collective-permute-start | bytes 6536 | tf_op jit(solution)/shard_map/ppermute | solution.py:45
  214.0 5.1 %reshape.47 = f32[3,32,2,32,2]{4,3,2,1,0:T(8,128)} reshape(f32[3,64,64]{2,1,0:T(8,128)} %fusion.80) | data formatting | bytes 98304 | tf_op jit(solution)/shard_map/reshape | solution.py:82
  219.1 3.0 reduce_sum.29
  226.1 5.9 %collective-permute-start.19 = (f32[3,32,1]{2,1,0:T(8,128)}, f32[3,32,1]{2,1,0:T(8,128)}, u32[]{:S(2)}, u32[]{:S(2)}) collective-permute-start(f32[3,32,1]{2,1,0:T(8,128)} %get-tuple-element.42), channel_id=1, source_target_pairs={{1,0},{2,1},{3,2},{4,3},{5,4},{6,5},{7,6},{8,7},{9,8},{10,9},{11,1... | collective-permute-start | bytes 1160 | tf_op jit(solution)/shard_map/ppermute | solution.py:24
  232.1 3.1 collective-permute-start.16
  235.2 2.7 collective-permute-start.17
  237.9 2.7 collective-permute-done.17
  243.9 5.8 %collective-permute-start.23 = (f32[3,32,1]{2,1,0:T(8,128)S(1)}, f32[3,32,1]{2,1,0:T(8,128)S(1)}, u32[]{:S(2)}, u32[]{:S(2)}) collective-permute-start(f32[3,32,1]{2,1,0:T(8,128)S(1)} %get-tuple-element.38), channel_id=1, source_target_pairs={{1,0},{2,1},{3,2},{4,3},{5,4},{6,5},{7,6},{8,7},{9,8},{10,9},{11,1... | collective-permute-start | bytes 1160 | tf_op jit(solution)/shard_map/ppermute | solution.py:24
  249.7 3.1 collective-permute-start.20
  252.8 2.7 collective-permute-start.21
  255.6 2.7 collective-permute-done.21
  261.3 5.8 %collective-permute-start.27 = (f32[3,32,1]{2,1,0:T(8,128)S(1)}, f32[3,32,1]{2,1,0:T(8,128)S(1)}, u32[]{:S(2)}, u32[]{:S(2)}) collective-permute-start(f32[3,32,1]{2,1,0:T(8,128)S(1)} %get-tuple-element.34), channel_id=1, source_target_pairs={{1,0},{2,1},{3,2},{4,3},{5,4},{6,5},{7,6},{8,7},{9,8},{10,9},{11,1... | collective-permute-start | bytes 1160 | tf_op jit(solution)/shard_map/ppermute | solution.py:24
  267.0 3.1 collective-permute-start.24
  270.2 2.7 collective-permute-start.25
  272.9 2.7 collective-permute-done.25
  282.9 3.1 collective-permute-start.28
  286.1 2.7 collective-permute-start.29
  288.8 2.8 collective-permute-done.29
  293.6 5.8 %collective-permute-start.31 = (f32[3,68,2]{2,1,0:T(8,128)S(1)}, f32[3,68,2]{2,1,0:T(8,128)S(1)}, u32[]{:S(2)}, u32[]{:S(2)}) collective-permute-start(f32[3,68,2]{2,1,0:T(8,128)S(1)} %get-tuple-element.28), channel_id=1, source_target_pairs={{1,0},{2,1},{3,2},{4,3},{5,4},{6,5},{7,6},{8,7},{9,8},{10,9},{11,1... | collective-permute-start | bytes 4904 | tf_op jit(solution)/shard_map/ppermute | solution.py:45
  308.7 3.1 collective-permute-start.32
  311.9 2.7 collective-permute-start.33
  314.6 2.8 collective-permute-done.33
  319.4 6.0 %collective-permute-start.35 = (f32[3,132,2]{2,1,0:T(8,128)S(1)}, f32[3,132,2]{2,1,0:T(8,128)S(1)}, u32[]{:S(2)}, u32[]{:S(2)}) collective-permute-start(f32[3,132,2]{2,1,0:T(8,128)S(1)} %get-tuple-element.20), channel_id=1, source_target_pairs={{1,0},{2,1},{3,2},{4,3},{5,4},{6,5},{7,6},{8,7},{9,8},{10,9},{11,1... | collective-permute-start | bytes 9512 | tf_op jit(solution)/shard_map/ppermute | solution.py:45
  332.9 2.6 mul.424
  337.4 3.1 collective-permute-start.36
  340.6 2.7 collective-permute-start.37
  343.3 3.8 %collective-permute-done.36 = f32[3,2,256]{1,2,0:T(8,128)S(1)} collective-permute-done((f32[3,2,256]{1,2,0:T(8,128)S(1)}, f32[3,2,256]{1,2,0:T(8,128)S(1)}, u32[]{:S(2)}, u32[]{:S(2)}) %collective-permute-start.36) | collective-permute-done | bytes 6176 | tf_op jit(solution)/shard_map/ppermute | solution.py:43
  347.1 3.1 collective-permute-done.37
  352.4 5.8 %collective-permute-start.39 = (f32[3,260,2]{1,2,0:T(2,128)S(1)}, f32[3,260,2]{1,2,0:T(2,128)S(1)}, u32[]{:S(2)}, u32[]{:S(2)}) collective-permute-start(f32[3,260,2]{1,2,0:T(2,128)S(1)} %get-tuple-element.12), channel_id=1, source_target_pairs={{1,0},{2,1},{3,2},{4,3},{5,4},{6,5},{7,6},{8,7},{9,8},{10,9},{11,1... | collective-permute-start | bytes 18728 | tf_op jit(solution)/shard_map/ppermute | solution.py:45
  364.0 2.3 copy.43
  (157 shorter events, 96.7 us)
Async XLA Ops:
  0.0 1.5 copy-start.13
  0.0 2.7 copy-start.14
  8.9 16.5 %collective-permute-start = (f32[9,1,256]{2,1,0:T(1,128)S(1)}, f32[9,1,256]{2,1,0:T(1,128)S(1)}, u32[]{:S(2)}, u32[]{:S(2)}) collective-permute-start(f32[9,1,256]{2,1,0:T(1,128)S(1)} %copy.30), channel_id=1, source_target_pairs={{0,32},{32,64},{64,96},{96,128},{128,160},{160,192},{192,224},{1,3... | collective-permute-start | bytes 27656 | tf_op jit(solution)/shard_map/ppermute | solution.py:23
  14.3 12.5 %collective-permute-start.1 = (f32[9,1,256]{2,1,0:T(1,128)S(1)}, f32[9,1,256]{2,1,0:T(1,128)S(1)}, u32[]{:S(2)}, u32[]{:S(2)}) collective-permute-start(f32[9,1,256]{2,1,0:T(1,128)S(1)} %copy.32), channel_id=1, source_target_pairs={{32,0},{64,32},{96,64},{128,96},{160,128},{192,160},{224,192},{33,... | collective-permute-start | bytes 27656 | tf_op jit(solution)/shard_map/ppermute | solution.py:24
  16.4 11.9 %collective-permute-start.2 = (f32[9,256,1]{1,2,0:T(1,128)S(1)}, f32[9,256,1]{1,2,0:T(1,128)S(1)}, u32[]{:S(2)}, u32[]{:S(2)}) collective-permute-start(f32[9,256,1]{1,2,0:T(1,128)S(1)} %get-tuple-element.5), channel_id=1, source_target_pairs={{0,1},{1,2},{2,3},{3,4},{4,5},{5,6},{6,7},{7,8},{8,9},{9,10},{10,1... | collective-permute-start | bytes 27656 | tf_op jit(solution)/shard_map/ppermute | solution.py:23
  18.3 10.0 %collective-permute-start.3 = (f32[9,256,1]{1,2,0:T(1,128)S(1)}, f32[9,256,1]{1,2,0:T(1,128)S(1)}, u32[]{:S(2)}, u32[]{:S(2)}) collective-permute-start(f32[9,256,1]{1,2,0:T(1,128)S(1)} %get-tuple-element.6), channel_id=1, source_target_pairs={{1,0},{2,1},{3,2},{4,3},{5,4},{6,5},{7,6},{8,7},{9,8},{10,9},{11,1... | collective-permute-start | bytes 27656 | tf_op jit(solution)/shard_map/ppermute | solution.py:24
  35.7 14.1 %collective-permute-start.4 = (f32[4,2,256]{1,2,0:T(8,128)S(1)}, f32[4,2,256]{1,2,0:T(8,128)S(1)}, u32[]{:S(2)}, u32[]{:S(2)}) collective-permute-start(f32[4,2,256]{1,2,0:T(8,128)S(1)} %get-tuple-element.15), channel_id=1, source_target_pairs={{0,32},{32,64},{64,96},{96,128},{128,160},{160,192},{192,224},{1,3... | collective-permute-start | bytes 24584 | tf_op jit(solution)/shard_map/ppermute | solution.py:43
  40.7 14.8 %collective-permute-start.5 = (f32[4,2,256]{1,2,0:T(8,128)S(1)}, f32[4,2,256]{1,2,0:T(8,128)S(1)}, u32[]{:S(2)}, u32[]{:S(2)}) collective-permute-start(f32[4,2,256]{1,2,0:T(8,128)S(1)} %get-tuple-element.16), channel_id=1, source_target_pairs={{32,0},{64,32},{96,64},{128,96},{160,128},{192,160},{224,192},{33,... | collective-permute-start | bytes 24584 | tf_op jit(solution)/shard_map/ppermute | solution.py:45
  55.6 7.7 %collective-permute-start.6 = (f32[4,260,2]{1,2,0:T(2,128)S(1)}, f32[4,260,2]{1,2,0:T(2,128)S(1)}, u32[]{:S(2)}, u32[]{:S(2)}) collective-permute-start(f32[4,260,2]{1,2,0:T(2,128)S(1)} %get-tuple-element.9), channel_id=1, source_target_pairs={{0,1},{1,2},{2,3},{3,4},{4,5},{5,6},{6,7},{7,8},{8,9},{9,10},{10,1... | collective-permute-start | bytes 24968 | tf_op jit(solution)/shard_map/ppermute | solution.py:43
  57.5 7.1 %collective-permute-start.7 = (f32[4,260,2]{1,2,0:T(2,128)S(1)}, f32[4,260,2]{1,2,0:T(2,128)S(1)}, u32[]{:S(2)}, u32[]{:S(2)}) collective-permute-start(f32[4,260,2]{1,2,0:T(2,128)S(1)} %get-tuple-element.10), channel_id=1, source_target_pairs={{1,0},{2,1},{3,2},{4,3},{5,4},{6,5},{7,6},{8,7},{9,8},{10,9},{11,1... | collective-permute-start | bytes 24968 | tf_op jit(solution)/shard_map/ppermute | solution.py:45
  65.5 2.6 copy-start.6
  145.0 6.8 %collective-permute-start.8 = (f32[4,2,128]{2,1,0:T(2,128)S(1)}, f32[4,2,128]{2,1,0:T(2,128)S(1)}, u32[]{:S(2)}, u32[]{:S(2)}) collective-permute-start(f32[4,2,128]{2,1,0:T(2,128)S(1)} %get-tuple-element.23), channel_id=1, source_target_pairs={{0,32},{32,64},{64,96},{96,128},{128,160},{160,192},{192,224},{1,3... | collective-permute-start | bytes 12296 | tf_op jit(solution)/shard_map/ppermute | solution.py:43
  149.9 5.5 %collective-permute-start.9 = (f32[4,2,128]{2,1,0:T(2,128)S(1)}, f32[4,2,128]{2,1,0:T(2,128)S(1)}, u32[]{:S(2)}, u32[]{:S(2)}) collective-permute-start(f32[4,2,128]{2,1,0:T(2,128)S(1)} %get-tuple-element.24), channel_id=1, source_target_pairs={{32,0},{64,32},{96,64},{128,96},{160,128},{192,160},{224,192},{33,... | collective-permute-start | bytes 12296 | tf_op jit(solution)/shard_map/ppermute | solution.py:45
  155.6 10.0 %collective-permute-start.10 = (f32[4,132,2]{2,1,0:T(8,128)S(1)}, f32[4,132,2]{2,1,0:T(8,128)S(1)}, u32[]{:S(2)}, u32[]{:S(2)}) collective-permute-start(f32[4,132,2]{2,1,0:T(8,128)S(1)} %get-tuple-element.17), channel_id=1, source_target_pairs={{0,1},{1,2},{2,3},{3,4},{4,5},{5,6},{6,7},{7,8},{8,9},{9,10},{10,1... | collective-permute-start | bytes 12680 | tf_op jit(solution)/shard_map/ppermute | solution.py:43
  157.5 9.8 %collective-permute-start.11 = (f32[4,132,2]{2,1,0:T(8,128)S(1)}, f32[4,132,2]{2,1,0:T(8,128)S(1)}, u32[]{:S(2)}, u32[]{:S(2)}) collective-permute-start(f32[4,132,2]{2,1,0:T(8,128)S(1)} %get-tuple-element.18), channel_id=1, source_target_pairs={{1,0},{2,1},{3,2},{4,3},{5,4},{6,5},{7,6},{8,7},{9,8},{10,9},{11,1... | collective-permute-start | bytes 12680 | tf_op jit(solution)/shard_map/ppermute | solution.py:45
  191.2 5.9 %collective-permute-start.12 = (f32[4,2,64]{2,1,0:T(2,128)S(1)}, f32[4,2,64]{2,1,0:T(2,128)S(1)}, u32[]{:S(2)}, u32[]{:S(2)}) collective-permute-start(f32[4,2,64]{2,1,0:T(2,128)S(1)} %get-tuple-element.31), channel_id=1, source_target_pairs={{0,32},{32,64},{64,96},{96,128},{128,160},{160,192},{192,224},{1,3... | collective-permute-start | bytes 6152 | tf_op jit(solution)/shard_map/ppermute | solution.py:43
  194.4 5.5 %collective-permute-start.13 = (f32[4,2,64]{2,1,0:T(2,128)S(1)}, f32[4,2,64]{2,1,0:T(2,128)S(1)}, u32[]{:S(2)}, u32[]{:S(2)}) collective-permute-start(f32[4,2,64]{2,1,0:T(2,128)S(1)} %get-tuple-element.32), channel_id=1, source_target_pairs={{32,0},{64,32},{96,64},{128,96},{160,128},{192,160},{224,192},{33,... | collective-permute-start | bytes 6152 | tf_op jit(solution)/shard_map/ppermute | solution.py:45
  197.1 3.6 copy-start.11
  200.7 8.9 %collective-permute-start.14 = (f32[4,68,2]{2,1,0:T(8,128)}, f32[4,68,2]{2,1,0:T(8,128)}, u32[]{:S(2)}, u32[]{:S(2)}) collective-permute-start(f32[4,68,2]{2,1,0:T(8,128)} %get-tuple-element.25), channel_id=1, source_target_pairs={{0,1},{1,2},{2,3},{3,4},{4,5},{5,6},{6,7},{7,8},{8,9},{9,10},{10,1... | collective-permute-start | bytes 6536 | tf_op jit(solution)/shard_map/ppermute | solution.py:43
  202.6 8.7 %collective-permute-start.15 = (f32[4,68,2]{2,1,0:T(8,128)}, f32[4,68,2]{2,1,0:T(8,128)}, u32[]{:S(2)}, u32[]{:S(2)}) collective-permute-start(f32[4,68,2]{2,1,0:T(8,128)} %get-tuple-element.26), channel_id=1, source_target_pairs={{1,0},{2,1},{3,2},{4,3},{5,4},{6,5},{7,6},{8,7},{9,8},{10,9},{11,1... | collective-permute-start | bytes 6536 | tf_op jit(solution)/shard_map/ppermute | solution.py:45
  224.2 13.7 %collective-permute-start.18 = (f32[3,32,1]{2,1,0:T(8,128)}, f32[3,32,1]{2,1,0:T(8,128)}, u32[]{:S(2)}, u32[]{:S(2)}) collective-permute-start(f32[3,32,1]{2,1,0:T(8,128)} %get-tuple-element.41), channel_id=1, source_target_pairs={{0,1},{1,2},{2,3},{3,4},{4,5},{5,6},{6,7},{7,8},{8,9},{9,10},{10,1... | collective-permute-start | bytes 1160 | tf_op jit(solution)/shard_map/ppermute | solution.py:23
  226.1 11.8 %collective-permute-start.19 = (f32[3,32,1]{2,1,0:T(8,128)}, f32[3,32,1]{2,1,0:T(8,128)}, u32[]{:S(2)}, u32[]{:S(2)}) collective-permute-start(f32[3,32,1]{2,1,0:T(8,128)} %get-tuple-element.42), channel_id=1, source_target_pairs={{1,0},{2,1},{3,2},{4,3},{5,4},{6,5},{7,6},{8,7},{9,8},{10,9},{11,1... | collective-permute-start | bytes 1160 | tf_op jit(solution)/shard_map/ppermute | solution.py:24
  232.1 5.9 %collective-permute-start.16 = (f32[3,1,32]{2,1,0:T(1,128)}, f32[3,1,32]{2,1,0:T(1,128)S(1)}, u32[]{:S(2)}, u32[]{:S(2)}) collective-permute-start(f32[3,1,32]{2,1,0:T(1,128)} %get-tuple-element.43), channel_id=1, source_target_pairs={{0,32},{32,64},{64,96},{96,128},{128,160},{160,192},{192,224},{1,3... | collective-permute-start | bytes 1160 | tf_op jit(solution)/shard_map/ppermute | solution.py:23
  235.2 5.5 %collective-permute-start.17 = (f32[3,1,32]{2,1,0:T(1,128)}, f32[3,1,32]{2,1,0:T(1,128)}, u32[]{:S(2)}, u32[]{:S(2)}) collective-permute-start(f32[3,1,32]{2,1,0:T(1,128)} %get-tuple-element.44), channel_id=1, source_target_pairs={{32,0},{64,32},{96,64},{128,96},{160,128},{192,160},{224,192},{33,... | collective-permute-start | bytes 1160 | tf_op jit(solution)/shard_map/ppermute | solution.py:24
  242.0 13.5 %collective-permute-start.22 = (f32[3,32,1]{2,1,0:T(8,128)S(1)}, f32[3,32,1]{2,1,0:T(8,128)S(1)}, u32[]{:S(2)}, u32[]{:S(2)}) collective-permute-start(f32[3,32,1]{2,1,0:T(8,128)S(1)} %get-tuple-element.37), channel_id=1, source_target_pairs={{0,1},{1,2},{2,3},{3,4},{4,5},{5,6},{6,7},{7,8},{8,9},{9,10},{10,1... | collective-permute-start | bytes 1160 | tf_op jit(solution)/shard_map/ppermute | solution.py:23
  243.9 11.6 %collective-permute-start.23 = (f32[3,32,1]{2,1,0:T(8,128)S(1)}, f32[3,32,1]{2,1,0:T(8,128)S(1)}, u32[]{:S(2)}, u32[]{:S(2)}) collective-permute-start(f32[3,32,1]{2,1,0:T(8,128)S(1)} %get-tuple-element.38), channel_id=1, source_target_pairs={{1,0},{2,1},{3,2},{4,3},{5,4},{6,5},{7,6},{8,7},{9,8},{10,9},{11,1... | collective-permute-start | bytes 1160 | tf_op jit(solution)/shard_map/ppermute | solution.py:24
  249.7 5.9 %collective-permute-start.20 = (f32[3,1,32]{2,1,0:T(1,128)S(1)}, f32[3,1,32]{2,1,0:T(1,128)S(1)}, u32[]{:S(2)}, u32[]{:S(2)}) collective-permute-start(f32[3,1,32]{2,1,0:T(1,128)S(1)} %get-tuple-element.39), channel_id=1, source_target_pairs={{0,32},{32,64},{64,96},{96,128},{128,160},{160,192},{192,224},{1,3... | collective-permute-start | bytes 1160 | tf_op jit(solution)/shard_map/ppermute | solution.py:23
  252.8 5.5 %collective-permute-start.21 = (f32[3,1,32]{2,1,0:T(1,128)S(1)}, f32[3,1,32]{2,1,0:T(1,128)S(1)}, u32[]{:S(2)}, u32[]{:S(2)}) collective-permute-start(f32[3,1,32]{2,1,0:T(1,128)S(1)} %get-tuple-element.40), channel_id=1, source_target_pairs={{32,0},{64,32},{96,64},{128,96},{160,128},{192,160},{224,192},{33,... | collective-permute-start | bytes 1160 | tf_op jit(solution)/shard_map/ppermute | solution.py:24
  259.3 13.5 %collective-permute-start.26 = (f32[3,32,1]{2,1,0:T(8,128)S(1)}, f32[3,32,1]{2,1,0:T(8,128)S(1)}, u32[]{:S(2)}, u32[]{:S(2)}) collective-permute-start(f32[3,32,1]{2,1,0:T(8,128)S(1)} %get-tuple-element.33), channel_id=1, source_target_pairs={{0,1},{1,2},{2,3},{3,4},{4,5},{5,6},{6,7},{7,8},{8,9},{9,10},{10,1... | collective-permute-start | bytes 1160 | tf_op jit(solution)/shard_map/ppermute | solution.py:23
  261.3 11.6 %collective-permute-start.27 = (f32[3,32,1]{2,1,0:T(8,128)S(1)}, f32[3,32,1]{2,1,0:T(8,128)S(1)}, u32[]{:S(2)}, u32[]{:S(2)}) collective-permute-start(f32[3,32,1]{2,1,0:T(8,128)S(1)} %get-tuple-element.34), channel_id=1, source_target_pairs={{1,0},{2,1},{3,2},{4,3},{5,4},{6,5},{7,6},{8,7},{9,8},{10,9},{11,1... | collective-permute-start | bytes 1160 | tf_op jit(solution)/shard_map/ppermute | solution.py:24
  267.0 5.9 %collective-permute-start.24 = (f32[3,1,32]{2,1,0:T(1,128)S(1)}, f32[3,1,32]{2,1,0:T(1,128)S(1)}, u32[]{:S(2)}, u32[]{:S(2)}) collective-permute-start(f32[3,1,32]{2,1,0:T(1,128)S(1)} %get-tuple-element.35), channel_id=1, source_target_pairs={{0,32},{32,64},{64,96},{96,128},{128,160},{160,192},{192,224},{1,3... | collective-permute-start | bytes 1160 | tf_op jit(solution)/shard_map/ppermute | solution.py:23
  270.2 5.5 %collective-permute-start.25 = (f32[3,1,32]{2,1,0:T(1,128)S(1)}, f32[3,1,32]{2,1,0:T(1,128)S(1)}, u32[]{:S(2)}, u32[]{:S(2)}) collective-permute-start(f32[3,1,32]{2,1,0:T(1,128)S(1)} %get-tuple-element.36), channel_id=1, source_target_pairs={{32,0},{64,32},{96,64},{128,96},{160,128},{192,160},{224,192},{33,... | collective-permute-start | bytes 1160 | tf_op jit(solution)/shard_map/ppermute | solution.py:24
  282.9 5.9 %collective-permute-start.28 = (f32[3,2,64]{2,1,0:T(2,128)S(1)}, f32[3,2,64]{2,1,0:T(2,128)S(1)}, u32[]{:S(2)}, u32[]{:S(2)}) collective-permute-start(f32[3,2,64]{2,1,0:T(2,128)S(1)} %get-tuple-element.29), channel_id=1, source_target_pairs={{0,32},{32,64},{64,96},{96,128},{128,160},{160,192},{192,224},{1,3... | collective-permute-start | bytes 4616 | tf_op jit(solution)/shard_map/ppermute | solution.py:43
  286.1 5.5 %collective-permute-start.29 = (f32[3,2,64]{2,1,0:T(2,128)S(1)}, f32[3,2,64]{2,1,0:T(2,128)S(1)}, u32[]{:S(2)}, u32[]{:S(2)}) collective-permute-start(f32[3,2,64]{2,1,0:T(2,128)S(1)} %get-tuple-element.30), channel_id=1, source_target_pairs={{32,0},{64,32},{96,64},{128,96},{160,128},{192,160},{224,192},{33,... | collective-permute-start | bytes 4616 | tf_op jit(solution)/shard_map/ppermute | solution.py:45
  291.7 8.2 %collective-permute-start.30 = (f32[3,68,2]{2,1,0:T(8,128)S(1)}, f32[3,68,2]{2,1,0:T(8,128)S(1)}, u32[]{:S(2)}, u32[]{:S(2)}) collective-permute-start(f32[3,68,2]{2,1,0:T(8,128)S(1)} %get-tuple-element.27), channel_id=1, source_target_pairs={{0,1},{1,2},{2,3},{3,4},{4,5},{5,6},{6,7},{7,8},{8,9},{9,10},{10,1... | collective-permute-start | bytes 4904 | tf_op jit(solution)/shard_map/ppermute | solution.py:43
  293.6 8.1 %collective-permute-start.31 = (f32[3,68,2]{2,1,0:T(8,128)S(1)}, f32[3,68,2]{2,1,0:T(8,128)S(1)}, u32[]{:S(2)}, u32[]{:S(2)}) collective-permute-start(f32[3,68,2]{2,1,0:T(8,128)S(1)} %get-tuple-element.28), channel_id=1, source_target_pairs={{1,0},{2,1},{3,2},{4,3},{5,4},{6,5},{7,6},{8,7},{9,8},{10,9},{11,1... | collective-permute-start | bytes 4904 | tf_op jit(solution)/shard_map/ppermute | solution.py:45
  307.4 21.3 %copy-start.4 = (f32[4,132,132]{2,1,0:T(8,128)S(1)}, f32[4,132,132]{2,1,0:T(8,128)}, u32[]{:S(2)}) copy-start(f32[4,132,132]{2,1,0:T(8,128)} %copy-done.3) | copy-start | bytes 836356
  307.4 21.3 %copy-start.10 = (f32[130,130]{1,0:T(8,128)S(1)}, f32[130,130]{1,0:T(8,128)}, u32[]{:S(2)}) copy-start(f32[130,130]{1,0:T(8,128)} %copy-done.9) | copy-start | bytes 202804
  308.7 5.9 %collective-permute-start.32 = (f32[3,2,128]{2,1,0:T(2,128)S(1)}, f32[3,2,128]{2,1,0:T(2,128)S(1)}, u32[]{:S(2)}, u32[]{:S(2)}) collective-permute-start(f32[3,2,128]{2,1,0:T(2,128)S(1)} %get-tuple-element.21), channel_id=1, source_target_pairs={{0,32},{32,64},{64,96},{96,128},{128,160},{160,192},{192,224},{1,3... | collective-permute-start | bytes 9224 | tf_op jit(solution)/shard_map/ppermute | solution.py:43
  311.9 5.5 %collective-permute-start.33 = (f32[3,2,128]{2,1,0:T(2,128)S(1)}, f32[3,2,128]{2,1,0:T(2,128)S(1)}, u32[]{:S(2)}, u32[]{:S(2)}) collective-permute-start(f32[3,2,128]{2,1,0:T(2,128)S(1)} %get-tuple-element.22), channel_id=1, source_target_pairs={{32,0},{64,32},{96,64},{128,96},{160,128},{192,160},{224,192},{33,... | collective-permute-start | bytes 9224 | tf_op jit(solution)/shard_map/ppermute | solution.py:45
  317.5 9.2 %collective-permute-start.34 = (f32[3,132,2]{2,1,0:T(8,128)S(1)}, f32[3,132,2]{2,1,0:T(8,128)S(1)}, u32[]{:S(2)}, u32[]{:S(2)}) collective-permute-start(f32[3,132,2]{2,1,0:T(8,128)S(1)} %get-tuple-element.19), channel_id=1, source_target_pairs={{0,1},{1,2},{2,3},{3,4},{4,5},{5,6},{6,7},{7,8},{8,9},{9,10},{10,1... | collective-permute-start | bytes 9512 | tf_op jit(solution)/shard_map/ppermute | solution.py:43
  319.4 9.1 %collective-permute-start.35 = (f32[3,132,2]{2,1,0:T(8,128)S(1)}, f32[3,132,2]{2,1,0:T(8,128)S(1)}, u32[]{:S(2)}, u32[]{:S(2)}) collective-permute-start(f32[3,132,2]{2,1,0:T(8,128)S(1)} %get-tuple-element.20), channel_id=1, source_target_pairs={{1,0},{2,1},{3,2},{4,3},{5,4},{6,5},{7,6},{8,7},{9,8},{10,9},{11,1... | collective-permute-start | bytes 9512 | tf_op jit(solution)/shard_map/ppermute | solution.py:45
  337.4 9.7 %collective-permute-start.36 = (f32[3,2,256]{1,2,0:T(8,128)S(1)}, f32[3,2,256]{1,2,0:T(8,128)S(1)}, u32[]{:S(2)}, u32[]{:S(2)}) collective-permute-start(f32[3,2,256]{1,2,0:T(8,128)S(1)} %get-tuple-element.13), channel_id=1, source_target_pairs={{0,32},{32,64},{64,96},{96,128},{128,160},{160,192},{192,224},{1,3... | collective-permute-start | bytes 18440 | tf_op jit(solution)/shard_map/ppermute | solution.py:43
  340.6 9.7 %collective-permute-start.37 = (f32[3,2,256]{1,2,0:T(8,128)S(1)}, f32[3,2,256]{1,2,0:T(8,128)S(1)}, u32[]{:S(2)}, u32[]{:S(2)}) collective-permute-start(f32[3,2,256]{1,2,0:T(8,128)S(1)} %get-tuple-element.14), channel_id=1, source_target_pairs={{32,0},{64,32},{96,64},{128,96},{160,128},{192,160},{224,192},{33,... | collective-permute-start | bytes 18440 | tf_op jit(solution)/shard_map/ppermute | solution.py:45
  350.3 9.7 %copy-start.2 = (f32[4,260,260]{1,2,0:T(8,128)S(1)}, f32[4,260,260]{1,2,0:T(8,128)}, u32[]{:S(2)}) copy-start(f32[4,260,260]{1,2,0:T(8,128)} %copy-done.1) | copy-start | bytes 3244804
  350.4 9.7 %copy-start.7 = (f32[258,258]{0,1:T(8,128)S(1)}, f32[258,258]{0,1:T(8,128)}, u32[]{:S(2)}) copy-start(f32[258,258]{0,1:T(8,128)} %copy-done.6) | copy-start | bytes 798772
  350.4 7.8 %collective-permute-start.38 = (f32[3,260,2]{1,2,0:T(2,128)S(1)}, f32[3,260,2]{1,2,0:T(2,128)S(1)}, u32[]{:S(2)}, u32[]{:S(2)}) collective-permute-start(f32[3,260,2]{1,2,0:T(2,128)S(1)} %get-tuple-element.11), channel_id=1, source_target_pairs={{0,1},{1,2},{2,3},{3,4},{4,5},{5,6},{6,7},{7,8},{8,9},{9,10},{10,1... | collective-permute-start | bytes 18728 | tf_op jit(solution)/shard_map/ppermute | solution.py:43
  352.4 7.1 %collective-permute-start.39 = (f32[3,260,2]{1,2,0:T(2,128)S(1)}, f32[3,260,2]{1,2,0:T(2,128)S(1)}, u32[]{:S(2)}, u32[]{:S(2)}) collective-permute-start(f32[3,260,2]{1,2,0:T(2,128)S(1)} %get-tuple-element.12), channel_id=1, source_target_pairs={{1,0},{2,1},{3,2},{4,3},{5,4},{6,5},{7,6},{8,7},{9,8},{10,9},{11,1... | collective-permute-start | bytes 18728 | tf_op jit(solution)/shard_map/ppermute | solution.py:45
  (8 other events, 6.4 us)
where the time goes:
time: 372 us; the launch traced here: 366 us
  starting transfers between devices  138 us (37%)
  local copies, waits for them, and re-layouts  110 us (30%)
  other arithmetic  61.6 us (17%)
  waiting for transfers between devices  54.7 us (15%)
    reshape x3, local copies, waits for them, and re-layouts, shrink(): return field.reshape(chans, rows // 2, 2, cols // 2, 2).mean(axis=(2, 4))  72.2 us
    ppermute x12, starting transfers between devices, padded_3(): lax.ppermute(head, axis, [((i + 1) % count, i) for i in range(ends)])  49.6 us
    ppermute x12, starting transfers between devices, padded_3(): lax.ppermute(tail, axis, [(i, (i + 1) % count) for i in range(ends)])  34 us
    ppermute x8, starting transfers between devices, padded_2(): lax.ppermute(leading, axis, [(b, a) for a, b in up])  33.3 us
    ppermute x12, waiting for transfers between devices, padded_3(): lax.ppermute(head, axis, [((i + 1) % count, i) for i in range(ends)])  30.4 us
    reduce_sum x3, other arithmetic, shrink(): return field.reshape(chans, rows // 2, 2, cols // 2, 2).mean(axis=(2, 4))  28.6 us
    ppermute x8, starting transfers between devices, padded_2(): lax.ppermute(last, axis, up)  20.9 us
    ppermute x12, waiting for transfers between devices, padded_3(): lax.ppermute(tail, axis, [(i, (i + 1) % count) for i in range(ends)])  16.1 us
  transfers between devices with their start and end apart: 40, of which 21 were waited for; matrix products, arithmetic and copies ran while one was open for 1% of the time, Pallas kernels for 0%

commit v1 on v0

v1 whole, which is shorter than its diff:
```python
import functools

import jax
import jax.numpy as jnp
from jax import lax
from jax.experimental import pallas as pl
from jax.experimental.pallas import tpu as pltpu
from jax.sharding import PartitionSpec as P

MESH = pl.DeviceIdType.MESH
F32 = jnp.float32
CHAN = 3
BS = 256
LANES = 128
HALO = 16
ROWS0 = BS + 2 * HALO + 16
ROWS1 = BS // 2 + HALO + 16
ROWS2 = BS // 4 + 2 * HALO + 16
ROWS3 = BS // 8 + HALO + 16
OWN0 = 8 + HALO
OWN1 = 16
OWN2 = 8 + HALO
OWN3 = 16
NEIGHBOURS = ((-1, 1), (-1, -1), (1, 1), (1, -1), (0, 1), (0, -1), (-1, 0), (1, 0))


def tile(base):
    return pl.ds(pl.multiple_of(base, 8), 8)


def beside(ref, slabs, base, lane):
    centre = [ref[s, tile(base), :] for s in slabs]
    column = [ref[s, pl.ds(base - 1, 8), :] + ref[s, pl.ds(base + 1, 8), :] for s in slabs]
    right = [pltpu.roll(c, LANES - 1, 1) for c in centre]
    left = [pltpu.roll(c, 1, 1) for c in centre]
    n = len(slabs)
    if n > 1:
        right = [jnp.where(lane == LANES - 1, right[(i + 1) % n], right[i]) for i in range(n)]
        left = [jnp.where(lane == 0, left[(i - 1) % n], left[i]) for i in range(n)]
    return centre, [column[i] + (left[i] + right[i]) for i in range(n)]


def take(x, index):
    return jnp.take_along_axis(x, index, axis=1)


def kernel(groups, blks, a_hbm, b_hbm, x_hbm, cov, lab, out,
           a_in, b_in, x_in, d, dh, pe, pw, hw, he, mask, labels,
           s0, v0, w0, s1, v1, w1, s2, pe2, pw2, hw2, he2, s2x, v2, w2, s3, v3, w3,
           in_sem, send1, recv1, send2, recv2):
    g, k = lax.axis_index("group"), lax.axis_index("blk")
    lane = lax.broadcasted_iota(jnp.int32, (8, LANES), 1)
    zeros = jnp.zeros((8, LANES), F32)

    loads = [
        pltpu.make_async_copy(src, dst, in_sem.at[i])
        for i, (src, dst) in enumerate(((a_hbm, a_in), (b_hbm, b_in), (x_hbm, x_in)))
    ]
    for copy in loads:
        copy.start()

    def there(dg, dk):
        ok = None
        for at, step, size in ((g, dg, groups), (k, dk, blks)):
            if step:
                good = at < size - 1 if step > 0 else at > 0
                ok = good if ok is None else jnp.logical_and(ok, good)
        return ok

    for slab in range(13):
        for base in (8, 16, BS + OWN0, BS + OWN0 + 8):
            d[slab, base:base + 8, :] = zeros
    for ref in (hw, he):
        @pl.loop(0, ROWS0 // 8)
        def _(i):
            ref[tile(8 * i), :] = zeros
    for ref in (hw2, he2):
        for base in range(0, ROWS2, 8):
            ref[base:base + 8, :] = zeros
    for c in range(CHAN):
        for base in (8, 16, BS // 4 + OWN2, BS // 4 + OWN2 + 8):
            s2[c, base:base + 8, :] = zeros
    for ref, rows in ((s0, ROWS0), (v0, ROWS0), (w0, ROWS0), (s1, ROWS1), (v1, ROWS1), (w1, ROWS1),
                      (s2x, ROWS2), (v2, ROWS2), (w2, ROWS2), (s3, ROWS3), (v3, ROWS3), (w3, ROWS3),
                      (d, ROWS0), (dh, ROWS0)):
        for slab in range(ref.shape[0]):
            ref[slab, 0:8, :] = zeros
            ref[slab, rows - 8:rows, :] = zeros

    barrier = pltpu.get_barrier_semaphore()
    count = jnp.int32(0)
    for dg, dk in NEIGHBOURS:
        ok = there(dg, dk)
        count = count + ok.astype(jnp.int32)

        @pl.when(ok)
        def _():
            pl.semaphore_signal(barrier, inc=1, device_id=(g + dg, k + dk), device_id_type=MESH)

    my_cov = jnp.full((8, LANES), cov[0, 0].astype(F32), F32)
    my_lab = jnp.full((8, LANES), lab[0, 0].astype(F32), F32)
    for base in (OWN0, BS + OWN0 - HALO):
        d[12, base:base + 8, :] = my_lab
        d[12, base + 8:base + 16, :] = my_cov
    meta = jnp.where(lane < 112, my_lab, my_cov)

    for copy in loads:
        copy.wait()

    @pl.loop(0, BS // 8)
    def _(i):
        rows, to = tile(8 * i), tile(OWN0 + 8 * i)
        right, left = meta, meta
        for c in range(CHAN):
            for t in range(2):
                cols = slice(LANES * t, LANES * (t + 1))
                x = x_in[c, rows, cols]
                for f, ref in enumerate((a_in, b_in)):
                    field = f * CHAN + c
                    diff = ref[c, rows, cols] - x
                    d[2 * field + t, to, :] = diff
                    here = jnp.logical_and(lane >= 16 * field, lane < 16 * field + 16)
                    if t == 0:
                        left = jnp.where(here, pltpu.roll(diff, 16 * field, 1), left)
                    else:
                        right = jnp.where(here, pltpu.roll(diff, (16 * field + 16) % LANES, 1), right)
        pe[rows, :] = right
        pw[rows, :] = left

    pl.semaphore_wait(barrier, count)

    def exchange(main, east, west, from_w, from_e, own, size, send, recv):
        n, top, low = HALO, own - HALO, own + size
        src_dst = {
            (-1, 1): (east.at[0:n], from_w.at[low:low + n]),
            (-1, -1): (west.at[0:n], from_e.at[low:low + n]),
            (1, 1): (east.at[size - n:size], from_w.at[top:top + n]),
            (1, -1): (west.at[size - n:size], from_e.at[top:top + n]),
            (0, 1): (east, from_w.at[own:own + size]),
            (0, -1): (west, from_e.at[own:own + size]),
            (-1, 0): (main.at[:, own:own + n, :], main.at[:, low:low + n, :]),
            (1, 0): (main.at[:, low - n:low, :], main.at[:, top:top + n, :]),
        }

        def copy_to(i, dg, dk):
            src, dst = src_dst[dg, dk]
            return pltpu.make_async_remote_copy(
                src_ref=src, dst_ref=dst, send_sem=send.at[i], recv_sem=recv.at[i],
                device_id=(g + dg, k + dk), device_id_type=MESH)

        for i, (dg, dk) in enumerate(NEIGHBOURS):
            @pl.when(there(dg, dk))
            def _():
                copy_to(i, dg, dk).start()

        def finish():
            for i, (dg, dk) in enumerate(NEIGHBOURS):
                @pl.when(there(-dg, -dk))
                def _():
                    copy_to(i, dg, dk).wait_recv()
            for i, (dg, dk) in enumerate(NEIGHBOURS):
                @pl.when(there(dg, dk))
                def _():
                    copy_to(i, dg, dk).wait_send()

        return finish

    exchange(d, pe, pw, hw, he, OWN0, BS, send1, recv1)()

    for z, base in enumerate((8, OWN0, BS + OWN0)):
        west, east = hw[base:base + 8, :], he[base:base + 8, :]
        at = lambda where: jnp.full((8, LANES), where, jnp.int32)
        lab_w, cov_w = take(west, at(96)), take(west, at(112))
        lab_e, cov_e = take(east, at(96)), take(east, at(112))
        lab_z, cov_z = (my_lab, my_cov) if z == 1 else (d[12, base:base + 8, :], d[12, base + 8:base + 16, :])
        mask[z, 0] = cov_z
        mask[z, 1] = jnp.where(lane < 64, cov_e, cov_w)
        mask[z, 2] = jnp.where(lane < 64, cov_z, jnp.where(lane < 96, cov_e, cov_w))
        mask[z, 3] = jnp.where(lane < 32, cov_z, jnp.where(lane < 80, cov_e, cov_w))
        labels[z, 0] = lab_z
        labels[z, 1] = jnp.where(lane < 64, lab_e, lab_w)

    def zone(i, before, own):
        return jnp.where(i < before, 0, jnp.where(i < before + own, 1, 2))

    @pl.loop(1, ROWS0 // 8 - 1)
    def _(i):
        west, east = hw[tile(8 * i), :], he[tile(8 * i), :]
        for f in range(2 * CHAN):
            side = jnp.where(lane < 16, pltpu.roll(east, (LANES - 16 * f) % LANES, 1), 0.0)
            dh[f, tile(8 * i), :] = jnp.where(lane >= 112, pltpu.roll(west, 112 - 16 * f, 1), side)

    def slabs0(c):
        return [3 * c, 3 * c + 1, 3 * c + 2]

    tiles0 = ROWS0 // 8 - 2

    def beside_d(field, base):
        refs = [d.at[2 * field], d.at[2 * field + 1], dh.at[field]]
        centre = [r[tile(base), :] for r in refs]
        column = [r[pl.ds(base - 1, 8), :] + r[pl.ds(base + 1, 8), :] for r in refs]
        right = [pltpu.roll(x, LANES - 1, 1) for x in centre]
        left = [pltpu.roll(x, 1, 1) for x in centre]
        right = [jnp.where(lane == LANES - 1, right[(i + 1) % 3], right[i]) for i in range(3)]
        left = [jnp.where(lane == 0, left[(i - 1) % 3], left[i]) for i in range(3)]
        return [4.0 * centre[i] - (column[i] + (left[i] + right[i])) for i in range(3)]

    @pl.loop(0, tiles0)
    def _(i):
        z = zone(i, 2, 32)
        base = 8 + 8 * i
        for c in range(CHAN):
            la, lb = beside_d(c, base), beside_d(CHAN + c, base)
            for t in range(3):
                kind = t // 2
                s0[3 * c + t, tile(base), :] = mask[z, kind] * jnp.where(labels[z, kind] == 1.0, lb[t], la[t])

    def down(s, v, w, tiles, zones, kinds, slabs_of):
        @pl.loop(0, tiles)
        def _(i):
            z, base = zone(i, *zones), 8 + 8 * i
            act = [mask[z, kind] * 0.04 for kind in sorted(set(kinds))]
            first = min(kinds)
            for c in range(CHAN):
                slabs = slabs_of(c)
                centre, around = beside(s, slabs, base, lane)
                for j, slab in enumerate(slabs):
                    v[slab, tile(base), :] = act[kinds[j] - first] * (6.0 * centre[j] + around[j])

        @pl.loop(0, tiles)
        def _(i):
            z, base = zone(i, *zones), 8 + 8 * i
            for c in range(CHAN):
                slabs = slabs_of(c)
                centre, around = beside(v, slabs, base, lane)
                for j, slab in enumerate(slabs):
                    w[slab, tile(base), :] = mask[z, kinds[j]] * (
                        s[slab, tile(base), :] + (around[j] - 4.0 * centre[j]))

    def sweep(s, v, w, start, tiles, zones, kinds, slabs_of):
        @pl.loop(start, start + tiles)
        def _(i):
            z, base = zone(i, *zones), 8 + 8 * i
            act = [mask[z, kind] * 0.2 for kind in sorted(set(kinds))]
            first = min(kinds)
            for c in range(CHAN):
                slabs = slabs_of(c)
                centre, around = beside(v, slabs, base, lane)
                for j, slab in enumerate(slabs):
                    w[slab, tile(base), :] = act[kinds[j] - first] * (
                        centre[j] + around[j] + s[slab, tile(base), :])

    def pair_rows(ref, slab, base):
        total = ref[slab, pl.ds(base, 8, stride=2), :] + ref[slab, pl.ds(base + 1, 8, stride=2), :]
        return total + pltpu.roll(total, LANES - 1, 1)

    twice = lax.rem(2 * lane, LANES)
    low, high = lane // 2, lane // 2 + 64

    down(s0, v0, w0, tiles0, (2, 32), (0, 0, 1), slabs0)

    tiles1 = ROWS1 // 8 - 2

    def slabs1(c):
        return [2 * c, 2 * c + 1]

    @pl.loop(0, tiles1)
    def _(i):
        fine, base = 8 + 16 * i, 8 + 8 * i
        for c in range(CHAN):
            x, y, h = (pair_rows(w0, 3 * c + t, fine) for t in range(3))
            s1[2 * c, tile(base), :] = jnp.where(lane < 64, take(x, twice), take(y, twice))
            s1[2 * c + 1, tile(base), :] = take(h, twice)

    down(s1, v1, w1, tiles1, (1, 16), (0, 1), slabs1)

    @pl.loop(0, BS // 32)
    def _(i):
        right, left = zeros, zeros
        for c in range(CHAN):
            x = take(pair_rows(w1, 2 * c, OWN1 + 16 * i), twice)
            s2[c, tile(OWN2 + 8 * i), :] = x
            here = jnp.logical_and(lane >= 16 * c, lane < 16 * c + 16)
            left = jnp.where(here, pltpu.roll(x, 16 * c, 1), left)
            right = jnp.where(here, pltpu.roll(x, (16 * c - 48) % LANES, 1), right)
        pe2[tile(8 * i), :] = right
        pw2[tile(8 * i), :] = left

    exchange(s2, pe2, pw2, hw2, he2, OWN2, BS // 4, send2, recv2)()

    tiles2 = ROWS2 // 8 - 2

    @pl.loop(0, tiles2)
    def _(i):
        rows = tile(8 + 8 * i)
        west, east = hw2[rows, :], he2[rows, :]
        for c in range(CHAN):
            side = jnp.where(lane < 80, pltpu.roll(east, (64 - 16 * c) % LANES, 1), 0.0)
            side = jnp.where(lane >= 112, pltpu.roll(west, 112 - 16 * c, 1), side)
            s2x[c, rows, :] = jnp.where(lane < 64, s2[c, rows, :], side)

    def slabs2(c):
        return [c]

    down(s2x, v2, w2, tiles2, (2, 8), (2,), slabs2)

    tiles3 = ROWS3 // 8 - 2

    @pl.loop(0, tiles3)
    def _(i):
        for c in range(CHAN):
            s3[c, tile(8 + 8 * i), :] = take(pair_rows(w2, c, 8 + 16 * i), twice)

    @pl.loop(0, tiles3)
    def _(i):
        z, base = zone(i, 1, 4), 8 + 8 * i
        for c in range(CHAN):
            (centre,), (around,) = beside(s3, [c], base, lane)
            v3[c, tile(base), :] = 0.04 * mask[z, 3] * (6.0 * centre + around)

    sweep(s3, v3, w3, 0, tiles3, (1, 4), (3,), slabs2)
    sweep(s3, w3, v3, 0, tiles3, (1, 4), (3,), slabs2)

    def add_up(v, slab, fine, act, value):
        for half in range(2):
            rows = pl.ds(fine + half, 8, stride=2)
            v[slab, rows, :] = v[slab, rows, :] + act * value

    @pl.loop(0, tiles3)
    def _(i):
        act = mask[zone(i, 1, 4), 2]
        for c in range(CHAN):
            value = v3[c, tile(8 + 8 * i), :]
            add_up(v2, c, 8 + 16 * i, act, take(value, jnp.where(lane < 96, low, high)))

    sweep(s2x, v2, w2, 0, tiles2, (2, 8), (2,), slabs2)
    sweep(s2x, w2, v2, 0, tiles2, (2, 8), (2,), slabs2)

    @pl.loop(0, ROWS1 // 16)
    def _(i):
        z = zone(i, 1, 8)
        for c in range(CHAN):
            value = v2[c, tile(OWN2 - 8 + 8 * i), :]
            add_up(v1, 2 * c, 16 * i, mask[z, 0], take(value, low))
            add_up(v1, 2 * c + 1, 16 * i, mask[z, 1], take(value, high))

    sweep(s1, v1, w1, 0, tiles1, (1, 16), (0, 1), slabs1)
    sweep(s1, w1, v1, 0, tiles1, (1, 16), (0, 1), slabs1)

    @pl.loop(0, tiles1)
    def _(i):
        z, fine = zone(i, 1, 16), 8 + 16 * i
        for c in range(CHAN):
            value, beyond = v1[2 * c, tile(8 + 8 * i), :], v1[2 * c + 1, tile(8 + 8 * i), :]
            add_up(v0, 3 * c, fine, mask[z, 0], take(value, low))
            add_up(v0, 3 * c + 1, fine, mask[z, 0], take(value, high))
            add_up(v0, 3 * c + 2, fine, mask[z, 1], take(beyond, jnp.where(lane < 64, low, high)))

    sweep(s0, v0, w0, 1, tiles0 - 2, (2, 32), (0, 0, 1), slabs0)

    act = mask[1, 0] * 0.2

    @pl.loop(0, BS // 8)
    def _(i):
        base = OWN0 + 8 * i
        for c in range(CHAN):
            centre, around = beside(w0, slabs0(c), base, lane)
            for t in range(2):
                cols = slice(LANES * t, LANES * (t + 1))
                out[c, tile(8 * i), cols] = x_in[c, tile(8 * i), cols] + act * (
                    centre[t] + around[t] + s0[3 * c + t, tile(base), :])


def shards(groups, blks, image_a, image_b, initial, coverage, seam_label):
    vmem = lambda *dims: pltpu.VMEM(dims, F32)
    image = vmem(CHAN, BS, BS)
    scratch = [image] * 3
    scratch += [vmem(13, ROWS0, LANES), vmem(6, ROWS0, LANES)]
    scratch += [vmem(BS, LANES)] * 2 + [vmem(ROWS0, LANES)] * 2
    scratch += [vmem(3, 4, 8, LANES), vmem(3, 2, 8, LANES)]
    scratch += [vmem(9, ROWS0, LANES)] * 3 + [vmem(6, ROWS1, LANES)] * 3
    scratch += [vmem(3, ROWS2, LANES)] + [vmem(BS // 4, LANES)] * 2 + [vmem(ROWS2, LANES)] * 2
    scratch += [vmem(3, ROWS2, LANES)] * 3 + [vmem(3, ROWS3, LANES)] * 3
    scratch += [pltpu.SemaphoreType.DMA((3,))] + [pltpu.SemaphoreType.DMA((8,))] * 4
    return pl.pallas_call(
        functools.partial(kernel, groups, blks),
        out_shape=jax.ShapeDtypeStruct(image_a.shape, F32),
        in_specs=[pl.BlockSpec(memory_space=pl.ANY)] * 3 + [pl.BlockSpec(memory_space=pltpu.SMEM)] * 2,
        out_specs=pl.BlockSpec(memory_space=pltpu.VMEM),
        scratch_shapes=scratch,
        compiler_params=pltpu.CompilerParams(
            collective_id=0, has_side_effects=True, vmem_limit_bytes=40 << 20),
    )(image_a, image_b, initial, coverage, seam_label)


def solution(mesh):
    placed = (P(None, "group", "blk"),) * 3 + (P("group", "blk"),) * 2
    return jax.shard_map(
        functools.partial(shards, mesh.shape["group"], mesh.shape["blk"]),
        mesh=mesh, in_specs=placed, out_specs=P(None, "group", "blk"), check_vma=False)
```

time: 372 us -> 61.7 us (0.17); the launches traced: 366 us -> 61.4 us
  starting transfers between devices: 138 us -> 0 us
  local copies, waits for them, and re-layouts: 110 us -> 4.27 us
  other arithmetic: 61.6 us -> 0 us
  Pallas kernels: 0 us -> 55.8 us
  waiting for transfers between devices: 54.7 us -> 0 us
    ppermute x40 -> x0, starting transfers between devices: 138 us -> none  [the longest x12 49.6 us: padded_3(): lax.ppermute(head, axis, [((i + 1) % count, i) for i in range(ends)])]
    reshape x3 -> x0, local copies, waits for them, and re-layouts: 72.2 us -> none  [shrink(): return field.reshape(chans, rows // 2, 2, cols // 2, 2).mean(axis=(2, 4))]
    pallas_call x0 -> x1, Pallas kernels: none -> 55.8 us  [shards(): pl.pallas_call(functools.partial(kernel, groups, blks), out_shape=jax.Sha...]
    ppermute x40 -> x0, waiting for transfers between devices: 54.7 us -> none  [the longest x12 30.4 us: padded_3(): lax.ppermute(head, axis, [((i + 1) % count, i) for i in range(ends)])]
    reduce_sum x3 -> x0, other arithmetic: 28.6 us -> none  [shrink(): return field.reshape(chans, rows // 2, 2, cols // 2, 2).mean(axis=(2, 4))]
    add x12 -> x0, other arithmetic: 14.5 us -> none  [the longest x6 6.39 us: wide_sweep(): inner + RELAX * active_in * (source_in - factor * (4.0 * inner - beside_s...]
    mul x7 -> x0, local copies, waits for them, and re-layouts: 11.8 us -> none  [the longest x6 9.49 us: deep_cycle(): approx = approx + active * expand(coarse_fix)]
    slice x20 -> x0, local copies, waits for them, and re-layouts: 8 us -> none  [the longest x9 4.92 us: padded_2(): last = lax.slice_in_dim(x, length - width, length, axis=dim)]
  transfers between devices with their start and end apart: 40 -> 0, of which waited for: 21 -> 0; matrix products, arithmetic and copies ran while one was open for 1% -> 0% of each run, Pallas kernels for 0% -> 0%
where the time goes in v1:
time: 61.7 us; the launch traced here: 61.4 us
  Pallas kernels  55.8 us (90%)
  local copies, waits for them, and re-layouts  4.27 us (7%)
  between operations  1.32 us (2%)
    pallas_call x1, Pallas kernels, shards(): pl.pallas_call(functools.partial(kernel, groups, blks), out_shape=jax.Sha...  55.8 us
    unnamed x7, local copies, waits for them, and re-layouts  4.27 us

profile of v1, /device:TPU:70, one launch (start us, length us, event | category | flops | bytes accessed | tf_op | source)
XLA Modules:
  0.0 61.4 jit_solution(14512263210339657649)
XLA Ops:
  1.3 0.0 copy-start
  1.3 1.1 %copy-done = f32[3,256,256]{2,1,0:T(8,128)S(1)} copy-done((f32[3,256,256]{2,1,0:T(8,128)S(1)}, f32[3,256,256]{2,1,0:T(8,128)}, u32[]{:S(2)}) %copy-start) | copy-done | bytes 786456
  2.4 0.0 copy-start.1
  2.4 1.1 %copy-done.1 = f32[3,256,256]{2,1,0:T(8,128)S(1)} copy-done((f32[3,256,256]{2,1,0:T(8,128)S(1)}, f32[3,256,256]{2,1,0:T(8,128)}, u32[]{:S(2)}) %copy-start.1) | copy-done | bytes 786456
  3.6 0.0 copy-start.2
  3.6 1.1 %copy-done.2 = f32[3,256,256]{2,1,0:T(8,128)S(1)} copy-done((f32[3,256,256]{2,1,0:T(8,128)S(1)}, f32[3,256,256]{2,1,0:T(8,128)}, u32[]{:S(2)}) %copy-start.2) | copy-done | bytes 786456
  4.7 55.8 %shard_map.55 = f32[3,256,256]{2,1,0:T(8,128)S(1)} custom-call(f32[3,256,256]{2,1,0:T(8,128)S(1)} %copy-done, f32[3,256,256]{2,1,0:T(8,128)S(1)} %copy-done.1, f32[3,256,256]{2,1,0:T(8,128)S(1)} %copy-done.2, s32[1,1]{1,0:T(1,128)S(6)} %copy.7.cov, s32[1,1]{1,0:T(1,128)S(6)} %copy.8.lab), custom_call_target="tpu_custom_call" | custom-call | tf_op jit(solution)/shard_map/pallas_call | solution.py:385
  60.6 0.9 %copy.9 = f32[3,256,256]{2,1,0:T(8,128)} copy(f32[3,256,256]{2,1,0:T(8,128)S(1)} %shard_map.55) | data formatting | bytes 1572864
Async XLA Ops:
  1.3 1.1 %copy-start = (f32[3,256,256]{2,1,0:T(8,128)S(1)}, f32[3,256,256]{2,1,0:T(8,128)}, u32[]{:S(2)}) copy-start(f32[3,256,256]{2,1,0:T(8,128)} %a_hbm.1) | copy-start | bytes 2359300
  2.4 1.1 %copy-start.1 = (f32[3,256,256]{2,1,0:T(8,128)S(1)}, f32[3,256,256]{2,1,0:T(8,128)}, u32[]{:S(2)}) copy-start(f32[3,256,256]{2,1,0:T(8,128)} %b_hbm.1) | copy-start | bytes 2359300
  3.6 1.1 %copy-start.2 = (f32[3,256,256]{2,1,0:T(8,128)S(1)}, f32[3,256,256]{2,1,0:T(8,128)}, u32[]{:S(2)}) copy-start(f32[3,256,256]{2,1,0:T(8,128)} %x_hbm.1) | copy-start | bytes 2359300

commit v2 on v1

--- a/solution.py
+++ b/solution.py
@@ -71,7 +71,7 @@
         for base in (8, 16, BS + OWN0, BS + OWN0 + 8):
             d[slab, base:base + 8, :] = zeros
     for ref in (hw, he):
-        @pl.loop(0, ROWS0 // 8)
+        @pl.loop(0, ROWS0 // 8, unroll=True)
         def _(i):
             ref[tile(8 * i), :] = zeros
     for ref in (hw2, he2):
@@ -107,7 +107,7 @@
     for copy in loads:
         copy.wait()
 
-    @pl.loop(0, BS // 8)
+    @pl.loop(0, BS // 8, unroll=True)
     def _(i):
         rows, to = tile(8 * i), tile(OWN0 + 8 * i)
         right, left = meta, meta
@@ -183,7 +183,7 @@
     def zone(i, before, own):
         return jnp.where(i < before, 0, jnp.where(i < before + own, 1, 2))
 
-    @pl.loop(1, ROWS0 // 8 - 1)
+    @pl.loop(1, ROWS0 // 8 - 1, unroll=True)
     def _(i):
         west, east = hw[tile(8 * i), :], he[tile(8 * i), :]
         for f in range(2 * CHAN):
@@ -205,7 +205,7 @@
         left = [jnp.where(lane == 0, left[(i - 1) % 3], left[i]) for i in range(3)]
         return [4.0 * centre[i] - (column[i] + (left[i] + right[i])) for i in range(3)]
 
-    @pl.loop(0, tiles0)
+    @pl.loop(0, tiles0, unroll=True)
     def _(i):
         z = zone(i, 2, 32)
         base = 8 + 8 * i
@@ -216,7 +216,7 @@
                 s0[3 * c + t, tile(base), :] = mask[z, kind] * jnp.where(labels[z, kind] == 1.0, lb[t], la[t])
 
     def down(s, v, w, tiles, zones, kinds, slabs_of):
-        @pl.loop(0, tiles)
+        @pl.loop(0, tiles, unroll=True)
         def _(i):
             z, base = zone(i, *zones), 8 + 8 * i
             act = [mask[z, kind] * 0.04 for kind in sorted(set(kinds))]
@@ -227,7 +227,7 @@
                 for j, slab in enumerate(slabs):
                     v[slab, tile(base), :] = act[kinds[j] - first] * (6.0 * centre[j] + around[j])
 
-        @pl.loop(0, tiles)
+        @pl.loop(0, tiles, unroll=True)
         def _(i):
             z, base = zone(i, *zones), 8 + 8 * i
             for c in range(CHAN):
@@ -238,7 +238,7 @@
                         s[slab, tile(base), :] + (around[j] - 4.0 * centre[j]))
 
     def sweep(s, v, w, start, tiles, zones, kinds, slabs_of):
-        @pl.loop(start, start + tiles)
+        @pl.loop(start, start + tiles, unroll=True)
         def _(i):
             z, base = zone(i, *zones), 8 + 8 * i
             act = [mask[z, kind] * 0.2 for kind in sorted(set(kinds))]
@@ -264,7 +264,7 @@
     def slabs1(c):
         return [2 * c, 2 * c + 1]
 
-    @pl.loop(0, tiles1)
+    @pl.loop(0, tiles1, unroll=True)
     def _(i):
         fine, base = 8 + 16 * i, 8 + 8 * i
         for c in range(CHAN):
@@ -274,7 +274,7 @@
 
     down(s1, v1, w1, tiles1, (1, 16), (0, 1), slabs1)
 
-    @pl.loop(0, BS // 32)
+    @pl.loop(0, BS // 32, unroll=True)
     def _(i):
         right, left = zeros, zeros
         for c in range(CHAN):
@@ -290,7 +290,7 @@
 
     tiles2 = ROWS2 // 8 - 2
 
-    @pl.loop(0, tiles2)
+    @pl.loop(0, tiles2, unroll=True)
     def _(i):
         rows = tile(8 + 8 * i)
         west, east = hw2[rows, :], he2[rows, :]
@@ -306,12 +306,12 @@
 
     tiles3 = ROWS3 // 8 - 2
 
-    @pl.loop(0, tiles3)
+    @pl.loop(0, tiles3, unroll=True)
     def _(i):
         for c in range(CHAN):
             s3[c, tile(8 + 8 * i), :] = take(pair_rows(w2, c, 8 + 16 * i), twice)
 
-    @pl.loop(0, tiles3)
+    @pl.loop(0, tiles3, unroll=True)
     def _(i):
         z, base = zone(i, 1, 4), 8 + 8 * i
         for c in range(CHAN):
@@ -326,7 +326,7 @@
             rows = pl.ds(fine + half, 8, stride=2)
             v[slab, rows, :] = v[slab, rows, :] + act * value
 
-    @pl.loop(0, tiles3)
+    @pl.loop(0, tiles3, unroll=True)
     def _(i):
         act = mask[zone(i, 1, 4), 2]
         for c in range(CHAN):
@@ -336,7 +336,7 @@
     sweep(s2x, v2, w2, 0, tiles2, (2, 8), (2,), slabs2)
     sweep(s2x, w2, v2, 0, tiles2, (2, 8), (2,), slabs2)
 
-    @pl.loop(0, ROWS1 // 16)
+    @pl.loop(0, ROWS1 // 16, unroll=True)
     def _(i):
         z = zone(i, 1, 8)
         for c in range(CHAN):
@@ -347,7 +347,7 @@
     sweep(s1, v1, w1, 0, tiles1, (1, 16), (0, 1), slabs1)
     sweep(s1, w1, v1, 0, tiles1, (1, 16), (0, 1), slabs1)
 
-    @pl.loop(0, tiles1)
+    @pl.loop(0, tiles1, unroll=True)
     def _(i):
         z, fine = zone(i, 1, 16), 8 + 16 * i
         for c in range(CHAN):
@@ -360,7 +360,7 @@
 
     act = mask[1, 0] * 0.2
 
-    @pl.loop(0, BS // 8)
+    @pl.loop(0, BS // 8, unroll=True)
     def _(i):
         base = OWN0 + 8 * i
         for c in range(CHAN):
@@ -389,7 +389,7 @@
         out_specs=pl.BlockSpec(memory_space=pltpu.VMEM),
         scratch_shapes=scratch,
         compiler_params=pltpu.CompilerParams(
-            collective_id=0, has_side_effects=True, vmem_limit_bytes=40 << 20),
+            collective_id=0, has_side_effects=True, vmem_limit_bytes=60 << 20),
     )(image_a, image_b, initial, coverage, seam_label)
 
 

time: 61.7 us -> 30.5 us (0.49)
  Pallas kernels: 55.8 us -> 27 us
  local copies, waits for them, and re-layouts: 4.27 us -> 2.06 us
    pallas_call x1, Pallas kernels: 55.8 us -> 27 us  [shards(): pl.pallas_call(functools.partial(kernel, groups, blks), out_shape=jax.Sha...]
    unnamed x7 -> x1, local copies, waits for them, and re-layouts: 4.27 us -> 2.06 us
where the time goes in v2:
time: 30.5 us; the launch traced here: 30.3 us
  Pallas kernels  27 us (89%)
  local copies, waits for them, and re-layouts  2.06 us (7%)
  between operations  1.3 us (4%)
    pallas_call x1, Pallas kernels, shards(): pl.pallas_call(functools.partial(kernel, groups, blks), out_shape=jax.Sha...  27 us
    unnamed x1, local copies, waits for them, and re-layouts  2.06 us

profile of v2, /device:TPU:70, one launch (start us, length us, event | category | flops | bytes accessed | tf_op | source)
XLA Modules:
  0.0 30.3 jit_solution(2588348866887019189)
XLA Ops:
  1.3 27.0 %shard_map.55 = f32[3,256,256]{2,1,0:T(8,128)} custom-call(f32[3,256,256]{2,1,0:T(8,128)} %a_hbm.1, f32[3,256,256]{2,1,0:T(8,128)} %b_hbm.1, f32[3,256,256]{2,1,0:T(8,128)} %x_hbm.1, s32[1,1]{1,0:T(1,128)S(6)} %copy.7.cov, s32[1,1]{1,0:T(1,128)S(6)} %copy.8.lab), custom_call_target="tpu_custom_call" | custom-call | tf_op jit(solution)/shard_map/pallas_call | solution.py:385
  28.3 2.1 %copy.9 = f32[3,256,256]{2,1,0:T(8,128)} copy(f32[3,256,256]{2,1,0:T(8,128)} %shard_map.55) | data formatting | bytes 1572864

commit v3 on v2

--- a/solution.py
+++ b/solution.py
@@ -21,6 +21,8 @@
 OWN1 = 16
 OWN2 = 8 + HALO
 OWN3 = 16
+FROM_WEST = (0, 32, 64, 96, 16, 48)
+FROM_EAST = tuple(at + 16 for at in FROM_WEST)
 NEIGHBOURS = ((-1, 1), (-1, -1), (1, 1), (1, -1), (0, 1), (0, -1), (-1, 0), (1, 0))
 
 
@@ -28,16 +30,20 @@
     return pl.ds(pl.multiple_of(base, 8), 8)
 
 
-def beside(ref, slabs, base, lane):
+def sides(tiles, j, lane):
+    n, here = len(tiles), tiles[j]
+    after = here if n == 1 else jnp.where(lane == 0, tiles[(j + 1) % n], here)
+    before = here if n == 1 else jnp.where(lane == LANES - 1, tiles[j - 1], here)
+    return pltpu.roll(after, LANES - 1, 1) + pltpu.roll(before, 1, 1)
+
+
+def beside(ref, slabs, base, lane, count=None):
     centre = [ref[s, tile(base), :] for s in slabs]
-    column = [ref[s, pl.ds(base - 1, 8), :] + ref[s, pl.ds(base + 1, 8), :] for s in slabs]
-    right = [pltpu.roll(c, LANES - 1, 1) for c in centre]
-    left = [pltpu.roll(c, 1, 1) for c in centre]
-    n = len(slabs)
-    if n > 1:
-        right = [jnp.where(lane == LANES - 1, right[(i + 1) % n], right[i]) for i in range(n)]
-        left = [jnp.where(lane == 0, left[(i - 1) % n], left[i]) for i in range(n)]
-    return centre, [column[i] + (left[i] + right[i]) for i in range(n)]
+    around = []
+    for j, s in enumerate(slabs[:count]):
+        column = ref[s, pl.ds(base - 1, 8), :] + ref[s, pl.ds(base + 1, 8), :]
+        around.append(column + sides(centre, j, lane))
+    return centre, around
 
 
 def take(x, index):
@@ -52,12 +58,17 @@
     lane = lax.broadcasted_iota(jnp.int32, (8, LANES), 1)
     zeros = jnp.zeros((8, LANES), F32)
 
+    spans = ((0, HALO), (BS - HALO, BS), (HALO, BS // 2), (BS // 2, BS - HALO))
     loads = [
-        pltpu.make_async_copy(src, dst, in_sem.at[i])
-        for i, (src, dst) in enumerate(((a_hbm, a_in), (b_hbm, b_in), (x_hbm, x_in)))
+        [
+            pltpu.make_async_copy(src.at[:, lo:hi, :], dst.at[:, lo:hi, :], in_sem.at[n, i])
+            for i, (src, dst) in enumerate(((a_hbm, a_in), (b_hbm, b_in), (x_hbm, x_in)))
+        ]
+        for n, (lo, hi) in enumerate(spans)
     ]
-    for copy in loads:
-        copy.start()
+    for group in loads:
+        for copy in group:
+            copy.start()
 
     def there(dg, dk):
         ok = None
@@ -102,15 +113,12 @@
     for base in (OWN0, BS + OWN0 - HALO):
         d[12, base:base + 8, :] = my_lab
         d[12, base + 8:base + 16, :] = my_cov
-    meta = jnp.where(lane < 112, my_lab, my_cov)
-
-    for copy in loads:
-        copy.wait()
-
-    @pl.loop(0, BS // 8, unroll=True)
-    def _(i):
+    meta_e = jnp.where(lane < 96, my_lab, my_cov)
+    meta_w = jnp.where(lane < 96, my_lab, my_cov)
+
+    def differences(i):
         rows, to = tile(8 * i), tile(OWN0 + 8 * i)
-        right, left = meta, meta
+        right, left = meta_e, meta_w
         for c in range(CHAN):
             for t in range(2):
                 cols = slice(LANES * t, LANES * (t + 1))
@@ -119,15 +127,20 @@
                     field = f * CHAN + c
                     diff = ref[c, rows, cols] - x
                     d[2 * field + t, to, :] = diff
-                    here = jnp.logical_and(lane >= 16 * field, lane < 16 * field + 16)
+                    start = FROM_WEST[field] if t else FROM_EAST[field]
+                    here = jnp.logical_and(lane >= start, lane < start + 16)
                     if t == 0:
-                        left = jnp.where(here, pltpu.roll(diff, 16 * field, 1), left)
+                        left = jnp.where(here, pltpu.roll(diff, start % LANES, 1), left)
                     else:
-                        right = jnp.where(here, pltpu.roll(diff, (16 * field + 16) % LANES, 1), right)
+                        right = jnp.where(here, pltpu.roll(diff, (start + 16) % LANES, 1), right)
         pe[rows, :] = right
         pw[rows, :] = left
 
-    pl.semaphore_wait(barrier, count)
+    def load_and_subtract(ns):
+        for n in ns:
+            for copy in loads[n]:
+                copy.wait()
+            pl.loop(spans[n][0] // 8, spans[n][1] // 8, unroll=True)(differences)
 
     def exchange(main, east, west, from_w, from_e, own, size, send, recv):
         n, top, low = HALO, own - HALO, own + size
@@ -148,10 +161,12 @@
                 src_ref=src, dst_ref=dst, send_sem=send.at[i], recv_sem=recv.at[i],
                 device_id=(g + dg, k + dk), device_id_type=MESH)
 
-        for i, (dg, dk) in enumerate(NEIGHBOURS):
-            @pl.when(there(dg, dk))
-            def _():
-                copy_to(i, dg, dk).start()
+        def start(which):
+            for i, (dg, dk) in enumerate(NEIGHBOURS):
+                if (dg != 0) in which:
+                    @pl.when(there(dg, dk))
+                    def _():
+                        copy_to(i, dg, dk).start()
 
         def finish():
             for i, (dg, dk) in enumerate(NEIGHBOURS):
@@ -163,15 +178,21 @@
                 def _():
                     copy_to(i, dg, dk).wait_send()
 
-        return finish
-
-    exchange(d, pe, pw, hw, he, OWN0, BS, send1, recv1)()
+        return start, finish
+
+    start, finish = exchange(d, pe, pw, hw, he, OWN0, BS, send1, recv1)
+    load_and_subtract((0, 1))
+    pl.semaphore_wait(barrier, count)
+    start((True,))
+    load_and_subtract((2, 3))
+    start((False,))
+    finish()
 
     for z, base in enumerate((8, OWN0, BS + OWN0)):
         west, east = hw[base:base + 8, :], he[base:base + 8, :]
         at = lambda where: jnp.full((8, LANES), where, jnp.int32)
-        lab_w, cov_w = take(west, at(96)), take(west, at(112))
-        lab_e, cov_e = take(east, at(96)), take(east, at(112))
+        lab_w, cov_w = take(west, at(80)), take(west, at(112))
+        lab_e, cov_e = take(east, at(0)), take(east, at(96))
         lab_z, cov_z = (my_lab, my_cov) if z == 1 else (d[12, base:base + 8, :], d[12, base + 8:base + 16, :])
         mask[z, 0] = cov_z
         mask[z, 1] = jnp.where(lane < 64, cov_e, cov_w)
@@ -179,6 +200,7 @@
         mask[z, 3] = jnp.where(lane < 32, cov_z, jnp.where(lane < 80, cov_e, cov_w))
         labels[z, 0] = lab_z
         labels[z, 1] = jnp.where(lane < 64, lab_e, lab_w)
+        labels[z, 2] = jnp.where(lane < 64, lab_w, lab_e)
 
     def zone(i, before, own):
         return jnp.where(i < before, 0, jnp.where(i < before + own, 1, 2))
@@ -186,36 +208,36 @@
     @pl.loop(1, ROWS0 // 8 - 1, unroll=True)
     def _(i):
         west, east = hw[tile(8 * i), :], he[tile(8 * i), :]
+        even = lax.rem(lane // 16, 2) == 0
+        merged = jnp.where(even, west, east), jnp.where(even, east, west)
         for f in range(2 * CHAN):
-            side = jnp.where(lane < 16, pltpu.roll(east, (LANES - 16 * f) % LANES, 1), 0.0)
-            dh[f, tile(8 * i), :] = jnp.where(lane >= 112, pltpu.roll(west, 112 - 16 * f, 1), side)
+            dh[f, tile(8 * i), :] = pltpu.roll(merged[f // 4], (112 - FROM_WEST[f]) % LANES, 1)
 
     def slabs0(c):
         return [3 * c, 3 * c + 1, 3 * c + 2]
 
     tiles0 = ROWS0 // 8 - 2
 
-    def beside_d(field, base):
-        refs = [d.at[2 * field], d.at[2 * field + 1], dh.at[field]]
-        centre = [r[tile(base), :] for r in refs]
-        column = [r[pl.ds(base - 1, 8), :] + r[pl.ds(base + 1, 8), :] for r in refs]
-        right = [pltpu.roll(x, LANES - 1, 1) for x in centre]
-        left = [pltpu.roll(x, 1, 1) for x in centre]
-        right = [jnp.where(lane == LANES - 1, right[(i + 1) % 3], right[i]) for i in range(3)]
-        left = [jnp.where(lane == 0, left[(i - 1) % 3], left[i]) for i in range(3)]
-        return [4.0 * centre[i] - (column[i] + (left[i] + right[i])) for i in range(3)]
-
     @pl.loop(0, tiles0, unroll=True)
     def _(i):
         z = zone(i, 2, 32)
         base = 8 + 8 * i
-        for c in range(CHAN):
-            la, lb = beside_d(c, base), beside_d(CHAN + c, base)
+        is_b = [labels[z, kind] == 1.0 for kind in range(3)]
+        for c in range(CHAN):
+            other = CHAN + c
+            pairs = [(d.at[2 * c], d.at[2 * other]), (d.at[2 * c + 1], d.at[2 * other + 1]), (dh.at[c], dh.at[other])]
+
+            def pick(t, kind, rows):
+                return jnp.where(is_b[kind], pairs[t][1][rows, :], pairs[t][0][rows, :])
+
             for t in range(3):
                 kind = t // 2
-                s0[3 * c + t, tile(base), :] = mask[z, kind] * jnp.where(labels[z, kind] == 1.0, lb[t], la[t])
-
-    def down(s, v, w, tiles, zones, kinds, slabs_of):
+                centre = [pick(u, kind if kind == 0 or u == 2 else 2, tile(base)) for u in range(3)]
+                column = pick(t, kind, pl.ds(base - 1, 8)) + pick(t, kind, pl.ds(base + 1, 8))
+                s0[3 * c + t, tile(base), :] = mask[z, kind] * (
+                    4.0 * centre[t] - (column + sides(centre, t, lane)))
+
+    def down(s, v, w, tiles, zones, kinds, slabs_of, left_over, count=None):
         @pl.loop(0, tiles, unroll=True)
         def _(i):
             z, base = zone(i, *zones), 8 + 8 * i
@@ -227,13 +249,13 @@
                 for j, slab in enumerate(slabs):
                     v[slab, tile(base), :] = act[kinds[j] - first] * (6.0 * centre[j] + around[j])
 
-        @pl.loop(0, tiles, unroll=True)
+        @pl.loop(*left_over, unroll=True)
         def _(i):
             z, base = zone(i, *zones), 8 + 8 * i
             for c in range(CHAN):
                 slabs = slabs_of(c)
-                centre, around = beside(v, slabs, base, lane)
-                for j, slab in enumerate(slabs):
+                centre, around = beside(v, slabs, base, lane, count)
+                for j, slab in enumerate(slabs[:count]):
                     w[slab, tile(base), :] = mask[z, kinds[j]] * (
                         s[slab, tile(base), :] + (around[j] - 4.0 * centre[j]))
 
@@ -250,14 +272,20 @@
                     w[slab, tile(base), :] = act[kinds[j] - first] * (
                         centre[j] + around[j] + s[slab, tile(base), :])
 
+    def add_rows(ref, slab, base):
+        return ref[slab, pl.ds(base, 8, stride=2), :] + ref[slab, pl.ds(base + 1, 8, stride=2), :]
+
     def pair_rows(ref, slab, base):
-        total = ref[slab, pl.ds(base, 8, stride=2), :] + ref[slab, pl.ds(base + 1, 8, stride=2), :]
+        total = add_rows(ref, slab, base)
         return total + pltpu.roll(total, LANES - 1, 1)
+
+    first = lax.rem(lane, 2) == 0
+    interleaved = jnp.where(lane < 64, 2 * lane, 2 * lane - (LANES - 1))
 
     twice = lax.rem(2 * lane, LANES)
     low, high = lane // 2, lane // 2 + 64
 
-    down(s0, v0, w0, tiles0, (2, 32), (0, 0, 1), slabs0)
+    down(s0, v0, w0, tiles0, (2, 32), (0, 0, 1), slabs0, (1, tiles0 - 1))
 
     tiles1 = ROWS1 // 8 - 2
 
@@ -268,11 +296,12 @@
     def _(i):
         fine, base = 8 + 16 * i, 8 + 8 * i
         for c in range(CHAN):
-            x, y, h = (pair_rows(w0, 3 * c + t, fine) for t in range(3))
-            s1[2 * c, tile(base), :] = jnp.where(lane < 64, take(x, twice), take(y, twice))
-            s1[2 * c + 1, tile(base), :] = take(h, twice)
-
-    down(s1, v1, w1, tiles1, (1, 16), (0, 1), slabs1)
+            x, y = (add_rows(w0, 3 * c + t, fine) for t in range(2))
+            pairs = jnp.where(first, x, pltpu.roll(y, 1, 1)) + jnp.where(first, pltpu.roll(x, LANES - 1, 1), y)
+            s1[2 * c, tile(base), :] = take(pairs, interleaved)
+            s1[2 * c + 1, tile(base), :] = take(pair_rows(w0, 3 * c + 2, fine), twice)
+
+    down(s1, v1, w1, tiles1, (1, 16), (0, 1), slabs1, (1, tiles1 - 1), 1)
 
     @pl.loop(0, BS // 32, unroll=True)
     def _(i):
@@ -286,7 +315,9 @@
         pe2[tile(8 * i), :] = right
         pw2[tile(8 * i), :] = left
 
-    exchange(s2, pe2, pw2, hw2, he2, OWN2, BS // 4, send2, recv2)()
+    start, finish = exchange(s2, pe2, pw2, hw2, he2, OWN2, BS // 4, send2, recv2)
+    start((True, False))
+    finish()
 
     tiles2 = ROWS2 // 8 - 2
 
@@ -302,7 +333,7 @@
     def slabs2(c):
         return [c]
 
-    down(s2x, v2, w2, tiles2, (2, 8), (2,), slabs2)
+    down(s2x, v2, w2, tiles2, (2, 8), (2,), slabs2, (0, tiles2))
 
     tiles3 = ROWS3 // 8 - 2
 
@@ -364,7 +395,7 @@
     def _(i):
         base = OWN0 + 8 * i
         for c in range(CHAN):
-            centre, around = beside(w0, slabs0(c), base, lane)
+            centre, around = beside(w0, slabs0(c), base, lane, 2)
             for t in range(2):
                 cols = slice(LANES * t, LANES * (t + 1))
                 out[c, tile(8 * i), cols] = x_in[c, tile(8 * i), cols] + act * (
@@ -377,20 +408,20 @@
     scratch = [image] * 3
     scratch += [vmem(13, ROWS0, LANES), vmem(6, ROWS0, LANES)]
     scratch += [vmem(BS, LANES)] * 2 + [vmem(ROWS0, LANES)] * 2
-    scratch += [vmem(3, 4, 8, LANES), vmem(3, 2, 8, LANES)]
+    scratch += [vmem(3, 4, 8, LANES), vmem(3, 3, 8, LANES)]
     scratch += [vmem(9, ROWS0, LANES)] * 3 + [vmem(6, ROWS1, LANES)] * 3
     scratch += [vmem(3, ROWS2, LANES)] + [vmem(BS // 4, LANES)] * 2 + [vmem(ROWS2, LANES)] * 2
     scratch += [vmem(3, ROWS2, LANES)] * 3 + [vmem(3, ROWS3, LANES)] * 3
-    scratch += [pltpu.SemaphoreType.DMA((3,))] + [pltpu.SemaphoreType.DMA((8,))] * 4
+    scratch += [pltpu.SemaphoreType.DMA((4, 3))] + [pltpu.SemaphoreType.DMA((8,))] * 4
     return pl.pallas_call(
         functools.partial(kernel, groups, blks),
-        out_shape=jax.ShapeDtypeStruct(image_a.shape, F32),
+        out_shape=pltpu.VMEM(image_a.shape, F32),
         in_specs=[pl.BlockSpec(memory_space=pl.ANY)] * 3 + [pl.BlockSpec(memory_space=pltpu.SMEM)] * 2,
         out_specs=pl.BlockSpec(memory_space=pltpu.VMEM),
         scratch_shapes=scratch,
         compiler_params=pltpu.CompilerParams(
-            collective_id=0, has_side_effects=True, vmem_limit_bytes=60 << 20),
-    )(image_a, image_b, initial, coverage, seam_label)
+            collective_id=0, has_side_effects=True, vmem_limit_bytes=40 << 20),
+    )(*(pltpu.with_memory_space_constraint(i, pltpu.HBM) for i in (image_a, image_b, initial)), coverage, seam_label)
 
 
 def solution(mesh):

time: 30.5 us -> 26.1 us (0.86)
  Pallas kernels: 27 us -> 23.8 us
  local copies, waits for them, and re-layouts: 2.06 us -> 0.88 us
    pallas_call x1, Pallas kernels: 27 us -> 23.8 us  [shards(): pl.pallas_call(functools.partial(kernel, groups, blks), out_shape=pltpu.V...]
    unnamed x1, local copies, waits for them, and re-layouts: 2.06 us -> 0.88 us
where the time goes in v3:
time: 26.1 us; the launch traced here: 26 us
  Pallas kernels  23.8 us (91%)
  between operations  1.3 us (5%)
  local copies, waits for them, and re-layouts  0.88 us (3%)
    pallas_call x1, Pallas kernels, shards(): pl.pallas_call(functools.partial(kernel, groups, blks), out_shape=pltpu.V...  23.8 us
    unnamed x1, local copies, waits for them, and re-layouts  0.88 us

profile of v3, /device:TPU:70, one launch (start us, length us, event | category | flops | bytes accessed | tf_op | source)
XLA Modules:
  0.0 26.0 jit_solution(12337297411558981866)
XLA Ops:
  1.3 23.8 %shard_map.55 = f32[3,256,256]{2,1,0:T(8,128)S(1)} custom-call(f32[3,256,256]{2,1,0:T(8,128)} %a_hbm.1, f32[3,256,256]{2,1,0:T(8,128)} %b_hbm.1, f32[3,256,256]{2,1,0:T(8,128)} %x_hbm.1, s32[1,1]{1,0:T(1,128)S(6)} %copy.8.cov, s32[1,1]{1,0:T(1,128)S(6)} %copy.9.lab), custom_call_target="tpu_custom_call" | custom-call | tf_op jit(solution)/shard_map/pallas_call | solution.py:416
  25.1 0.9 %copy.7 = f32[3,256,256]{2,1,0:T(8,128)} copy(f32[3,256,256]{2,1,0:T(8,128)S(1)} %shard_map.55) | data formatting | bytes 1572864

commit v4 on v3

--- a/solution.py
+++ b/solution.py
@@ -12,6 +12,7 @@
 CHAN = 3
 BS = 256
 LANES = 128
+SENT = 12
 HALO = 16
 ROWS0 = BS + 2 * HALO + 16
 ROWS1 = BS // 2 + HALO + 16
@@ -26,6 +27,9 @@
 NEIGHBOURS = ((-1, 1), (-1, -1), (1, 1), (1, -1), (0, 1), (0, -1), (-1, 0), (1, 0))
 
 
+SENDS = ((-1, 1), (-1, -1), (1, 1), (1, -1), (-1, 0), (1, 0), (0, 1, 0), (0, -1, 0), (0, 1, 1), (0, -1, 1))
+
+
 def tile(base):
     return pl.ds(pl.multiple_of(base, 8), 8)
 
@@ -46,8 +50,20 @@
     return centre, around
 
 
-def take(x, index):
-    return jnp.take_along_axis(x, index, axis=1)
+def move(x, lanes):
+    total = None
+    for _ in range(3):
+        part = x.astype(jnp.bfloat16)
+        x = x - part.astype(F32)
+        term = jnp.dot(part, lanes, preferred_element_type=F32)
+        total = term if total is None else total + term
+    return total
+
+
+def ones_where(shape, test):
+    k = lax.broadcasted_iota(jnp.int32, shape, 0)
+    l = lax.broadcasted_iota(jnp.int32, shape, 1)
+    return jnp.where(test(k, l), 1.0, 0.0).astype(jnp.bfloat16)
 
 
 def kernel(groups, blks, a_hbm, b_hbm, x_hbm, cov, lab, out,
@@ -143,57 +159,64 @@
             pl.loop(spans[n][0] // 8, spans[n][1] // 8, unroll=True)(differences)
 
     def exchange(main, east, west, from_w, from_e, own, size, send, recv):
-        n, top, low = HALO, own - HALO, own + size
+        n, top, low = SENT, own - SENT, own + size
         src_dst = {
             (-1, 1): (east.at[0:n], from_w.at[low:low + n]),
             (-1, -1): (west.at[0:n], from_e.at[low:low + n]),
             (1, 1): (east.at[size - n:size], from_w.at[top:top + n]),
             (1, -1): (west.at[size - n:size], from_e.at[top:top + n]),
-            (0, 1): (east, from_w.at[own:own + size]),
-            (0, -1): (west, from_e.at[own:own + size]),
+            (0, 1, 0): (east.at[0:size // 2], from_w.at[own:own + size // 2]),
+            (0, 1, 1): (east.at[size // 2:size], from_w.at[own + size // 2:own + size]),
+            (0, -1, 0): (west.at[0:size // 2], from_e.at[own:own + size // 2]),
+            (0, -1, 1): (west.at[size // 2:size], from_e.at[own + size // 2:own + size]),
             (-1, 0): (main.at[:, own:own + n, :], main.at[:, low:low + n, :]),
             (1, 0): (main.at[:, low - n:low, :], main.at[:, top:top + n, :]),
         }
 
-        def copy_to(i, dg, dk):
-            src, dst = src_dst[dg, dk]
+        def copy_to(i, dg, dk, *part):
+            src, dst = src_dst[(dg, dk, *part)]
             return pltpu.make_async_remote_copy(
                 src_ref=src, dst_ref=dst, send_sem=send.at[i], recv_sem=recv.at[i],
                 device_id=(g + dg, k + dk), device_id_type=MESH)
 
         def start(which):
-            for i, (dg, dk) in enumerate(NEIGHBOURS):
-                if (dg != 0) in which:
-                    @pl.when(there(dg, dk))
-                    def _():
-                        copy_to(i, dg, dk).start()
+            for i in which:
+                dg, dk, *part = SENDS[i]
+
+                @pl.when(there(dg, dk))
+                def _():
+                    copy_to(i, dg, dk, *part).start()
 
         def finish():
-            for i, (dg, dk) in enumerate(NEIGHBOURS):
+            for i, (dg, dk, *part) in enumerate(SENDS):
                 @pl.when(there(-dg, -dk))
                 def _():
-                    copy_to(i, dg, dk).wait_recv()
-            for i, (dg, dk) in enumerate(NEIGHBOURS):
+                    copy_to(i, dg, dk, *part).wait_recv()
+            for i, (dg, dk, *part) in enumerate(SENDS):
                 @pl.when(there(dg, dk))
                 def _():
-                    copy_to(i, dg, dk).wait_send()
+                    copy_to(i, dg, dk, *part).wait_send()
 
         return start, finish
 
     start, finish = exchange(d, pe, pw, hw, he, OWN0, BS, send1, recv1)
     load_and_subtract((0, 1))
     pl.semaphore_wait(barrier, count)
-    start((True,))
-    load_and_subtract((2, 3))
-    start((False,))
+    start(range(6))
+    load_and_subtract((2,))
+    start((6, 7))
+    load_and_subtract((3,))
+    start((8, 9))
     finish()
 
     for z, base in enumerate((8, OWN0, BS + OWN0)):
-        west, east = hw[base:base + 8, :], he[base:base + 8, :]
-        at = lambda where: jnp.full((8, LANES), where, jnp.int32)
-        lab_w, cov_w = take(west, at(80)), take(west, at(112))
-        lab_e, cov_e = take(east, at(0)), take(east, at(96))
-        lab_z, cov_z = (my_lab, my_cov) if z == 1 else (d[12, base:base + 8, :], d[12, base + 8:base + 16, :])
+        at_row = base + 8 if z == 0 else base
+        west, east = hw[at_row:at_row + 8, :], he[at_row:at_row + 8, :]
+        at = lambda x, where: jnp.broadcast_to(x[:, where:where + 1], (8, LANES))
+        lab_w, cov_w = at(west, 80), at(west, 112)
+        lab_e, cov_e = at(east, 0), at(east, 96)
+        lab_z, cov_z = (my_lab, my_cov) if z == 1 else tuple(
+            jnp.broadcast_to(d[12, row:row + 1, :], (8, LANES)) for row in (base + 7, base + 8))
         mask[z, 0] = cov_z
         mask[z, 1] = jnp.where(lane < 64, cov_e, cov_w)
         mask[z, 2] = jnp.where(lane < 64, cov_z, jnp.where(lane < 96, cov_e, cov_w))
@@ -272,18 +295,15 @@
                     w[slab, tile(base), :] = act[kinds[j] - first] * (
                         centre[j] + around[j] + s[slab, tile(base), :])
 
-    def add_rows(ref, slab, base):
-        return ref[slab, pl.ds(base, 8, stride=2), :] + ref[slab, pl.ds(base + 1, 8, stride=2), :]
-
-    def pair_rows(ref, slab, base):
-        total = add_rows(ref, slab, base)
-        return total + pltpu.roll(total, LANES - 1, 1)
-
-    first = lax.rem(lane, 2) == 0
-    interleaved = jnp.where(lane < 64, 2 * lane, 2 * lane - (LANES - 1))
-
-    twice = lax.rem(2 * lane, LANES)
-    low, high = lane // 2, lane // 2 + 64
+    def add_rows(ref, slab, base, rows):
+        return ref[slab, pl.ds(base, rows, stride=2), :] + ref[slab, pl.ds(base + 1, rows, stride=2), :]
+
+    square = (LANES, LANES)
+    halve = ones_where((2 * LANES, LANES), lambda k, l: k // 2 == l)
+    halve_one = ones_where(square, lambda k, l: k // 2 == lax.rem(l, 64))
+    double = ones_where((LANES, 2 * LANES), lambda k, l: k == l // 2)
+    double_sides = ones_where(square, lambda k, l: k == jnp.where(l < 64, l // 2, l // 2 + 64))
+    double_coarse = ones_where(square, lambda k, l: k == jnp.where(l < 96, l // 2, l // 2 + 64))
 
     down(s0, v0, w0, tiles0, (2, 32), (0, 0, 1), slabs0, (1, tiles0 - 1))
 
@@ -292,23 +312,22 @@
     def slabs1(c):
         return [2 * c, 2 * c + 1]
 
-    @pl.loop(0, tiles1, unroll=True)
-    def _(i):
-        fine, base = 8 + 16 * i, 8 + 8 * i
-        for c in range(CHAN):
-            x, y = (add_rows(w0, 3 * c + t, fine) for t in range(2))
-            pairs = jnp.where(first, x, pltpu.roll(y, 1, 1)) + jnp.where(first, pltpu.roll(x, LANES - 1, 1), y)
-            s1[2 * c, tile(base), :] = take(pairs, interleaved)
-            s1[2 * c + 1, tile(base), :] = take(pair_rows(w0, 3 * c + 2, fine), twice)
+    rows1 = 8 * tiles1
+    for c in range(CHAN):
+        middle = jnp.concatenate([add_rows(w0, 3 * c + t, 8, rows1) for t in range(2)], axis=1)
+        s1[2 * c, 8:8 + rows1, :] = move(middle, halve)
+        s1[2 * c + 1, 8:8 + rows1, :] = move(add_rows(w0, 3 * c + 2, 8, rows1), halve_one)
 
     down(s1, v1, w1, tiles1, (1, 16), (0, 1), slabs1, (1, tiles1 - 1), 1)
 
+    for c in range(CHAN):
+        s2[c, OWN2:OWN2 + BS // 4, :] = move(add_rows(w1, 2 * c, OWN1, BS // 4), halve_one)
+
     @pl.loop(0, BS // 32, unroll=True)
     def _(i):
         right, left = zeros, zeros
         for c in range(CHAN):
-            x = take(pair_rows(w1, 2 * c, OWN1 + 16 * i), twice)
-            s2[c, tile(OWN2 + 8 * i), :] = x
+            x = s2[c, tile(OWN2 + 8 * i), :]
             here = jnp.logical_and(lane >= 16 * c, lane < 16 * c + 16)
             left = jnp.where(here, pltpu.roll(x, 16 * c, 1), left)
             right = jnp.where(here, pltpu.roll(x, (16 * c - 48) % LANES, 1), right)
@@ -316,7 +335,7 @@
         pw2[tile(8 * i), :] = left
 
     start, finish = exchange(s2, pe2, pw2, hw2, he2, OWN2, BS // 4, send2, recv2)
-    start((True, False))
+    start(range(10))
     finish()
 
     tiles2 = ROWS2 // 8 - 2
@@ -337,10 +356,9 @@
 
     tiles3 = ROWS3 // 8 - 2
 
-    @pl.loop(0, tiles3, unroll=True)
-    def _(i):
-        for c in range(CHAN):
-            s3[c, tile(8 + 8 * i), :] = take(pair_rows(w2, c, 8 + 16 * i), twice)
+    rows3 = 8 * tiles3
+    for c in range(CHAN):
+        s3[c, 8:8 + rows3, :] = move(add_rows(w2, c, 8, rows3), halve_one)
 
     @pl.loop(0, tiles3, unroll=True)
     def _(i):
@@ -357,35 +375,46 @@
             rows = pl.ds(fine + half, 8, stride=2)
             v[slab, rows, :] = v[slab, rows, :] + act * value
 
+    for c in range(CHAN):
+        w3[c, 8:8 + rows3, :] = move(v3[c, 8:8 + rows3, :], double_coarse)
+
     @pl.loop(0, tiles3, unroll=True)
     def _(i):
         act = mask[zone(i, 1, 4), 2]
         for c in range(CHAN):
-            value = v3[c, tile(8 + 8 * i), :]
-            add_up(v2, c, 8 + 16 * i, act, take(value, jnp.where(lane < 96, low, high)))
+            add_up(v2, c, 8 + 16 * i, act, w3[c, tile(8 + 8 * i), :])
 
     sweep(s2x, v2, w2, 0, tiles2, (2, 8), (2,), slabs2)
     sweep(s2x, w2, v2, 0, tiles2, (2, 8), (2,), slabs2)
 
+    half1 = ROWS1 // 2
+    for c in range(CHAN):
+        both = move(v2[c, OWN2 - 8:OWN2 - 8 + half1, :], double)
+        for t in range(2):
+            w1[2 * c + t, 0:half1, :] = both[:, LANES * t:LANES * (t + 1)]
+
     @pl.loop(0, ROWS1 // 16, unroll=True)
     def _(i):
         z = zone(i, 1, 8)
         for c in range(CHAN):
-            value = v2[c, tile(OWN2 - 8 + 8 * i), :]
-            add_up(v1, 2 * c, 16 * i, mask[z, 0], take(value, low))
-            add_up(v1, 2 * c + 1, 16 * i, mask[z, 1], take(value, high))
+            for t in range(2):
+                add_up(v1, 2 * c + t, 16 * i, mask[z, t], w1[2 * c + t, tile(8 * i), :])
 
     sweep(s1, v1, w1, 0, tiles1, (1, 16), (0, 1), slabs1)
     sweep(s1, w1, v1, 0, tiles1, (1, 16), (0, 1), slabs1)
 
+    for c in range(CHAN):
+        both = move(v1[2 * c, 8:8 + rows1, :], double)
+        for t in range(2):
+            w0[3 * c + t, 8:8 + rows1, :] = both[:, LANES * t:LANES * (t + 1)]
+        w0[3 * c + 2, 8:8 + rows1, :] = move(v1[2 * c + 1, 8:8 + rows1, :], double_sides)
+
     @pl.loop(0, tiles1, unroll=True)
     def _(i):
-        z, fine = zone(i, 1, 16), 8 + 16 * i
-        for c in range(CHAN):
-            value, beyond = v1[2 * c, tile(8 + 8 * i), :], v1[2 * c + 1, tile(8 + 8 * i), :]
-            add_up(v0, 3 * c, fine, mask[z, 0], take(value, low))
-            add_up(v0, 3 * c + 1, fine, mask[z, 0], take(value, high))
-            add_up(v0, 3 * c + 2, fine, mask[z, 1], take(beyond, jnp.where(lane < 64, low, high)))
+        z = zone(i, 1, 16)
+        for c in range(CHAN):
+            for t in range(3):
+                add_up(v0, 3 * c + t, 8 + 16 * i, mask[z, t // 2], w0[3 * c + t, tile(8 + 8 * i), :])
 
     sweep(s0, v0, w0, 1, tiles0 - 2, (2, 32), (0, 0, 1), slabs0)
 
@@ -412,7 +441,7 @@
     scratch += [vmem(9, ROWS0, LANES)] * 3 + [vmem(6, ROWS1, LANES)] * 3
     scratch += [vmem(3, ROWS2, LANES)] + [vmem(BS // 4, LANES)] * 2 + [vmem(ROWS2, LANES)] * 2
     scratch += [vmem(3, ROWS2, LANES)] * 3 + [vmem(3, ROWS3, LANES)] * 3
-    scratch += [pltpu.SemaphoreType.DMA((4, 3))] + [pltpu.SemaphoreType.DMA((8,))] * 4
+    scratch += [pltpu.SemaphoreType.DMA((4, 3))] + [pltpu.SemaphoreType.DMA((len(SENDS),))] * 4
     return pl.pallas_call(
         functools.partial(kernel, groups, blks),
         out_shape=pltpu.VMEM(image_a.shape, F32),

time: 26.1 us -> 24.1 us (0.923)
  Pallas kernels: 23.8 us -> 21.8 us
    pallas_call x1, Pallas kernels: 23.8 us -> 21.8 us  [shards(): pl.pallas_call(functools.partial(kernel, groups, blks), out_shape=pltpu.V...]
where the time goes in v4:
time: 24.1 us; the launch traced here: 24 us
  Pallas kernels  21.8 us (90%)
  between operations  1.3 us (5%)
  local copies, waits for them, and re-layouts  0.88 us (4%)
    pallas_call x1, Pallas kernels, shards(): pl.pallas_call(functools.partial(kernel, groups, blks), out_shape=pltpu.V...  21.8 us
    unnamed x1, local copies, waits for them, and re-layouts  0.88 us

profile of v4, /device:TPU:70, one launch (start us, length us, event | category | flops | bytes accessed | tf_op | source)
XLA Modules:
  0.0 24.0 jit_solution(3455758728550674652)
XLA Ops:
  1.3 21.8 %shard_map.55 = f32[3,256,256]{2,1,0:T(8,128)S(1)} custom-call(f32[3,256,256]{2,1,0:T(8,128)} %a_hbm.1, f32[3,256,256]{2,1,0:T(8,128)} %b_hbm.1, f32[3,256,256]{2,1,0:T(8,128)} %x_hbm.1, s32[1,1]{1,0:T(1,128)S(6)} %copy.8.cov, s32[1,1]{1,0:T(1,128)S(6)} %copy.9.lab), custom_call_target="tpu_custom_call" | custom-call | tf_op jit(solution)/shard_map/pallas_call | solution.py:445
  23.1 0.9 %copy.7 = f32[3,256,256]{2,1,0:T(8,128)} copy(f32[3,256,256]{2,1,0:T(8,128)S(1)} %shard_map.55) | data formatting | bytes 1572864
